TPU v7x, 32 devices: a whole 2x2x4 slice. The times are simulated.
32 devices in a mesh: group: 8 (over y, x, core), rep: 4 (over z).
Axes of the slice: x: 2, y: 2, z: 4, core: 2. Of those that a mesh axis runs over, the one named last changes fastest.
Arguments:
- tokens: bfloat16 [8192, 768], P(('group', 'rep')), may hold values from -6 to 6
- segments: int32 [8192], P(('group', 'rep')), may hold values from -1 to 3, as said below
- attn_in_weight: bfloat16 [2, 768, 2304], P(None, 'group'), may hold values from -8 to 8
- attn_bias: bfloat16 [2, 3, 768], P(None, None, 'group'), may hold values from -1.75 to 1.75
- out_weight: bfloat16 [2, 768, 768], P(None, 'group'), may hold values from -0.875 to 0.875
- fc1_weight: bfloat16 [2, 768, 3072], P(None, 'group'), may hold values from -0.21875 to 0.21875
- fc1_bias: bfloat16 [2, 3072], P(None, 'group'), may hold values from -1.75 to 1.75
- fc2_weight: bfloat16 [2, 3072, 768], P(None, 'group'), may hold values from -0.109375 to 0.109375
- fc2_bias: bfloat16 [2, 768], P(None, 'group'), may hold values from -1.75 to 1.75
- ln_gain: bfloat16 [2, 2, 768], P(None, None, 'group'), may hold values from 0.25 to 1.75
- ln_bias: bfloat16 [2, 2, 768], P(None, None, 'group'), may hold values from -1.75 to 1.75
- cotangent: bfloat16 [8192, 768], P(('group', 'rep')), may hold values from -12 to 12
Outputs:
- output: float32 [8192, 768], P(('group', 'rep'))
- input_grad: float32 [8192, 768], P(('group', 'rep'))
- grad_attn_in: float32 [2, 768, 2304], P(None, 'group')
- grad_attn_bias: float32 [2, 3, 768], P(None, None, 'group')
- grad_out_weight: float32 [2, 768, 768], P(None, 'group')
- grad_fc1_weight: float32 [2, 768, 3072], P(None, 'group')
- grad_fc1_bias: float32 [2, 3072], P(None, 'group')
- grad_fc2_weight: float32 [2, 3072, 768], P(None, 'group')
- grad_fc2_bias: float32 [2, 768], P(None, 'group')
- grad_ln_gain: float32 [2, 2, 768], P(None, None, 'group')
- grad_ln_bias: float32 [2, 2, 768], P(None, None, 'group')
Inputs may be any that keep to these rules, and one draw needn't show every extreme that they name: `segments`: each clip occupies exactly 1500 consecutive positions, clip numbers rise by one along the tokens, the first clip starts at the first token, padding elsewhere.
All inputs are finite; a program needn't handle non-finite values.
Results may differ from a plain program's by a relative error of at most 0.017.
Values may be sent and summed in bfloat16 or wider, within the bound.
No kernel may reach another device: no remote copies, remote signals or barrier semaphores. Data moves between devices by JAX's collectives and lax.ppermute only.
A program may use at most 256 MiB of HBM per device.

v0:
```python
import jax
import jax.numpy as jnp
from jax import lax
from jax.sharding import PartitionSpec as P

H = 12
HD = 64
LAYERS = 2
REACH = 6


EPSILON = 1e-05


def passed_along(value, axis, steps):
    count = lax.axis_size(axis)
    leading, last = (max(0, -steps), min(count, count - steps))
    return lax.ppermute(value, axis, [(source, source + steps) for source in range(leading, last)])


def layer_norm(values, gain, offset):
    center = jnp.mean(values, axis=-1, keepdims=True)
    shifted = values - center
    spread = jnp.mean(shifted * shifted, axis=-1, keepdims=True)
    inverse = lax.rsqrt(spread + EPSILON)
    unit_rows = shifted * inverse
    return (unit_rows * gain.astype(jnp.float32) + offset.astype(jnp.float32), unit_rows, inverse)


def norm_back(upstream, unit_rows, inverse, gain):
    scaled = upstream * gain.astype(jnp.float32)
    result = inverse * (
        scaled
        - jnp.mean(scaled, axis=-1, keepdims=True)
        - unit_rows * jnp.mean(scaled * unit_rows, axis=-1, keepdims=True)
    )
    return (result, jnp.sum(upstream * unit_rows, axis=0), jnp.sum(upstream, axis=0))


def gelu_slope(inputs):
    normal_cdf = 0.5 * (1.0 + lax.erf(inputs * 0.7071067811865476))
    return normal_cdf + inputs * jnp.exp(-0.5 * inputs * inputs) * 0.3989422804014327


def split_heads(matrix):
    return matrix.reshape(matrix.shape[0], H // 2, 2, HD).transpose(1, 0, 2, 3)


def join_heads(stacked):
    return stacked.transpose(1, 0, 2, 3).reshape(stacked.shape[1], H * HD)


def head_forward(queries, key_block, value_block, allowed):
    scores = jnp.einsum("qhd,khd->hqk", queries, key_block, preferred_element_type=jnp.float32)
    scores = jnp.where(allowed[None], scores, -1e30)
    top_score = jnp.max(scores, axis=2, keepdims=True)
    expd = jnp.exp(scores - top_score)
    total = jnp.sum(expd, axis=2, keepdims=True)
    probs = (expd / total).astype(jnp.bfloat16)
    heard = jnp.einsum("hqk,khd->qhd", probs, value_block, preferred_element_type=jnp.float32)
    return (heard, top_score[:, :, 0] + jnp.log(total[:, :, 0]))


def head_backward(queries, key_block, value_block, allowed, log_totals, upstream):
    scores = jnp.einsum("qhd,khd->hqk", queries, key_block, preferred_element_type=jnp.float32)
    probs = jnp.where(allowed[None], jnp.exp(scores - log_totals[:, :, None]), 0.0)
    rounded = probs.astype(jnp.bfloat16)
    d_value = jnp.einsum("hqk,qhd->khd", rounded, upstream, preferred_element_type=jnp.float32)
    d_probs = jnp.einsum("qhd,khd->hqk", upstream, value_block, preferred_element_type=jnp.float32)
    delta = jnp.sum(probs * d_probs, axis=2, keepdims=True)
    d_scores = (probs * (d_probs - delta)).astype(jnp.bfloat16)
    d_query = jnp.einsum("hqk,khd->qhd", d_scores, key_block, preferred_element_type=jnp.float32)
    d_key = jnp.einsum("hqk,qhd->khd", d_scores, queries, preferred_element_type=jnp.float32)
    return (d_query, d_key, d_value)


def local(
    tokens,
    segments,
    attn_in_weight,
    attn_bias,
    out_weight,
    fc1_weight,
    fc1_bias,
    fc2_weight,
    fc2_bias,
    ln_gain,
    ln_bias,
    cotangent,
):
    tok_rows = tokens.shape[0]
    width = H * HD
    score_scale = HD ** (-0.5)
    labels = segments + 2
    own_place = lax.iota(jnp.int32, tok_rows) + REACH * tok_rows
    window_place = lax.iota(jnp.int32, (2 * REACH + 1) * tok_rows)
    resid = tokens.astype(jnp.float32)
    fetched = []
    every_store = []
    for layer_at in range(LAYERS):
        weights = (
            lax.all_gather(attn_in_weight[layer_at], "group", axis=0, tiled=True),
            lax.all_gather(attn_bias[layer_at], "group", axis=1, tiled=True),
            lax.all_gather(out_weight[layer_at], "group", axis=0, tiled=True),
            lax.all_gather(fc1_weight[layer_at], "group", axis=0, tiled=True),
            lax.all_gather(fc1_bias[layer_at], "group", axis=0, tiled=True),
            lax.all_gather(fc2_weight[layer_at], "group", axis=0, tiled=True),
            lax.all_gather(fc2_bias[layer_at], "group", axis=0, tiled=True),
            lax.all_gather(ln_gain[layer_at], "group", axis=1, tiled=True),
            lax.all_gather(ln_bias[layer_at], "group", axis=1, tiled=True),
        )
        (
            forward_w_in,
            forward_b_attn,
            forward_w_out,
            forward_w_up,
            forward_b_up,
            forward_w_down,
            forward_b_down,
            forward_gains,
            forward_offsets,
        ) = weights
        normed, forward_unit_first, forward_inverse_first = layer_norm(
            resid, forward_gains[0], forward_offsets[0]
        )
        forward_first = normed.astype(jnp.bfloat16)
        mixed = jnp.dot(forward_first, forward_w_in, preferred_element_type=jnp.float32)
        forward_queries = (
            (mixed[:, :width] + forward_b_attn[0].astype(jnp.float32)) * score_scale
        ).astype(jnp.bfloat16)
        forward_key_value = jnp.concatenate(
            [
                mixed[:, width : 2 * width],
                mixed[:, 2 * width :] + forward_b_attn[1].astype(jnp.float32),
            ],
            axis=1,
        ).astype(jnp.bfloat16)
        lower_parts = []
        upper_parts = []
        for gather_distance in range(1, REACH + 1):
            lower_parts.append(
                passed_along((forward_key_value, labels), ("group", "rep"), gather_distance)
            )
            upper_parts.append(
                passed_along((forward_key_value, labels), ("group", "rep"), -gather_distance)
            )
        ordered = lower_parts[::-1] + [(forward_key_value, labels)] + upper_parts
        window_rows = jnp.concatenate([member[0] for member in ordered], axis=0)
        window_labels = jnp.concatenate([member[1] for member in ordered], axis=0)
        same = labels[:, None] == window_labels[None, :]
        forward_allowed = same & (
            (labels[:, None] >= 2) | (own_place[:, None] == window_place[None, :])
        )

        def attend_pair(members):
            return head_forward(members[0], members[1], members[2], forward_allowed)

        attended, forward_log_totals = lax.map(
            attend_pair,
            (
                split_heads(forward_queries),
                split_heads(window_rows[:, :width]),
                split_heads(window_rows[:, width:]),
            ),
        )
        forward_heard = join_heads(attended).astype(jnp.bfloat16)
        middle = (
            resid
            + jnp.dot(forward_heard, forward_w_out, preferred_element_type=jnp.float32)
            + forward_b_attn[2].astype(jnp.float32)
        )
        normed_two, forward_unit_second, forward_inverse_second = layer_norm(
            middle, forward_gains[1], forward_offsets[1]
        )
        forward_second = normed_two.astype(jnp.bfloat16)
        forward_pre_act = jnp.dot(
            forward_second, forward_w_up, preferred_element_type=jnp.float32
        ) + forward_b_up.astype(jnp.float32)
        forward_active = jax.nn.gelu(forward_pre_act, approximate=False).astype(jnp.bfloat16)
        result = (
            middle
            + jnp.dot(forward_active, forward_w_down, preferred_element_type=jnp.float32)
            + forward_b_down.astype(jnp.float32)
        )
        forward_stored = (
            forward_unit_first,
            forward_inverse_first,
            forward_first,
            forward_queries,
            window_rows,
            forward_allowed,
            forward_heard,
            forward_log_totals,
            forward_unit_second,
            forward_inverse_second,
            forward_second,
            forward_pre_act,
            forward_active,
        )
        resid = result
        fetched.append(None)
        every_store.append(forward_stored)
    upstream = cotangent.astype(jnp.float32)
    shares = [None] * LAYERS
    for layer_at in reversed(range(LAYERS)):
        weights = (
            lax.all_gather(attn_in_weight[layer_at], "group", axis=0, tiled=True),
            lax.all_gather(attn_bias[layer_at], "group", axis=1, tiled=True),
            lax.all_gather(out_weight[layer_at], "group", axis=0, tiled=True),
            lax.all_gather(fc1_weight[layer_at], "group", axis=0, tiled=True),
            lax.all_gather(fc1_bias[layer_at], "group", axis=0, tiled=True),
            lax.all_gather(fc2_weight[layer_at], "group", axis=0, tiled=True),
            lax.all_gather(fc2_bias[layer_at], "group", axis=0, tiled=True),
            lax.all_gather(ln_gain[layer_at], "group", axis=1, tiled=True),
            lax.all_gather(ln_bias[layer_at], "group", axis=1, tiled=True),
        )
        w_in, b_attn, w_out, w_up, b_up, w_down, b_down, gains, offsets = weights
        (
            unit_first,
            inverse_first,
            first,
            queries,
            window_kv,
            allowed,
            heard,
            log_totals,
            unit_second,
            inverse_second,
            second,
            pre_act,
            active,
        ) = every_store[layer_at]
        down_rounded = upstream.astype(jnp.bfloat16)
        g_down_b = jnp.sum(upstream, axis=0)
        g_down_w = jnp.einsum("tf,td->fd", active, down_rounded, preferred_element_type=jnp.float32)
        d_pre = jnp.einsum(
            "td,fd->tf", down_rounded, w_down, preferred_element_type=jnp.float32
        ) * gelu_slope(pre_act)
        up_rounded = d_pre.astype(jnp.bfloat16)
        g_up_b = jnp.sum(d_pre, axis=0)
        g_up_w = jnp.einsum("td,tf->df", second, up_rounded, preferred_element_type=jnp.float32)
        d_second = jnp.einsum("tf,df->td", up_rounded, w_up, preferred_element_type=jnp.float32)
        d_norm_two, g_gain_two, g_offset_two = norm_back(
            d_second, unit_second, inverse_second, gains[1]
        )
        d_middle = upstream + d_norm_two
        middle_rounded = d_middle.astype(jnp.bfloat16)
        g_out_b = jnp.sum(d_middle, axis=0)
        g_out_w = jnp.einsum("td,te->de", heard, middle_rounded, preferred_element_type=jnp.float32)
        d_heard = jnp.einsum(
            "te,de->td", middle_rounded, w_out, preferred_element_type=jnp.float32
        ).astype(jnp.bfloat16)

        def pair_backward(members):
            return head_backward(
                members[0], members[1], members[2], allowed, members[3], members[4]
            )

        d_query, d_key, d_value = lax.map(
            pair_backward,
            (
                split_heads(queries),
                split_heads(window_kv[:, :width]),
                split_heads(window_kv[:, width:]),
                log_totals,
                split_heads(d_heard),
            ),
        )
        d_window = jnp.concatenate([join_heads(d_key), join_heads(d_value)], axis=1)
        d_own = d_window[REACH * tok_rows : (REACH + 1) * tok_rows]
        for distance in range(1, REACH + 1):
            lower_block = d_window[
                (REACH - distance) * tok_rows : (REACH - distance + 1) * tok_rows
            ]
            upper_block = d_window[
                (REACH + distance) * tok_rows : (REACH + distance + 1) * tok_rows
            ]
            d_own = d_own + passed_along(
                lower_block.astype(jnp.bfloat16), ("group", "rep"), -distance
            ).astype(lower_block.dtype)
            d_own = d_own + passed_along(
                upper_block.astype(jnp.bfloat16), ("group", "rep"), distance
            ).astype(upper_block.dtype)
        d_queries = join_heads(d_query) * score_scale
        d_mixed = jnp.concatenate([d_queries, d_own], axis=1)
        mixed_rounded = d_mixed.astype(jnp.bfloat16)
        g_attn_b = jnp.stack(
            [jnp.sum(d_queries, axis=0), jnp.sum(d_own[:, width:], axis=0), g_out_b]
        )
        g_in_w = jnp.einsum("td,te->de", first, mixed_rounded, preferred_element_type=jnp.float32)
        d_first = jnp.einsum("te,de->td", mixed_rounded, w_in, preferred_element_type=jnp.float32)
        d_norm_one, g_gain_one, g_offset_one = norm_back(
            d_first, unit_first, inverse_first, gains[0]
        )
        d_resid = d_middle + d_norm_one
        grads = (
            g_in_w,
            g_attn_b,
            g_out_w,
            g_up_w,
            g_up_b,
            g_down_w,
            g_down_b,
            jnp.stack([g_gain_one, g_gain_two]),
            jnp.stack([g_offset_one, g_offset_two]),
        )
        upstream, grads = (d_resid, grads)
        summed = (
            lax.psum_scatter(
                grads[0].astype(jnp.bfloat16), "group", scatter_dimension=0, tiled=True
            ).astype(jnp.float32),
            lax.psum_scatter(
                grads[1].astype(jnp.bfloat16), "group", scatter_dimension=1, tiled=True
            ).astype(jnp.float32),
            lax.psum_scatter(
                grads[2].astype(jnp.bfloat16), "group", scatter_dimension=0, tiled=True
            ).astype(jnp.float32),
            lax.psum_scatter(
                grads[3].astype(jnp.bfloat16), "group", scatter_dimension=0, tiled=True
            ).astype(jnp.float32),
            lax.psum_scatter(
                grads[4].astype(jnp.bfloat16), "group", scatter_dimension=0, tiled=True
            ).astype(jnp.float32),
            lax.psum_scatter(
                grads[5].astype(jnp.bfloat16), "group", scatter_dimension=0, tiled=True
            ).astype(jnp.float32),
            lax.psum_scatter(
                grads[6].astype(jnp.bfloat16), "group", scatter_dimension=0, tiled=True
            ).astype(jnp.float32),
            lax.psum_scatter(
                grads[7].astype(jnp.bfloat16), "group", scatter_dimension=1, tiled=True
            ).astype(jnp.float32),
            lax.psum_scatter(
                grads[8].astype(jnp.bfloat16), "group", scatter_dimension=1, tiled=True
            ).astype(jnp.float32),
        )
        summed = (
            lax.psum(summed[0].astype(jnp.bfloat16), "rep").astype(jnp.float32),
            lax.psum(summed[1].astype(jnp.bfloat16), "rep").astype(jnp.float32),
            lax.psum(summed[2].astype(jnp.bfloat16), "rep").astype(jnp.float32),
            lax.psum(summed[3].astype(jnp.bfloat16), "rep").astype(jnp.float32),
            lax.psum(summed[4].astype(jnp.bfloat16), "rep").astype(jnp.float32),
            lax.psum(summed[5].astype(jnp.bfloat16), "rep").astype(jnp.float32),
            lax.psum(summed[6].astype(jnp.bfloat16), "rep").astype(jnp.float32),
            lax.psum(summed[7].astype(jnp.bfloat16), "rep").astype(jnp.float32),
            lax.psum(summed[8].astype(jnp.bfloat16), "rep").astype(jnp.float32),
        )
        shares[layer_at] = summed
    stacked = [
        jnp.stack([shares[layer_at][field] for layer_at in range(LAYERS)]) for field in range(9)
    ]
    return (
        resid,
        upstream,
        stacked[0],
        stacked[1],
        stacked[2],
        stacked[3],
        stacked[4],
        stacked[5],
        stacked[6],
        stacked[7],
        stacked[8],
    )


def solution(mesh):
    in_specs = (
        P(("group", "rep"), None),
        P(("group", "rep")),
        P(None, "group", None),
        P(None, None, "group"),
        P(None, "group", None),
        P(None, "group", None),
        P(None, "group"),
        P(None, "group", None),
        P(None, "group"),
        P(None, None, "group"),
        P(None, None, "group"),
        P(("group", "rep"), None),
    )
    out_specs = (
        P(("group", "rep"), None),
        P(("group", "rep"), None),
        P(None, "group", None),
        P(None, None, "group"),
        P(None, "group", None),
        P(None, "group", None),
        P(None, "group"),
        P(None, "group", None),
        P(None, "group"),
        P(None, None, "group"),
        P(None, None, "group"),
    )
    return jax.shard_map(local, mesh=mesh, in_specs=in_specs, out_specs=out_specs, check_vma=False)
```

profile of v0, /device:TPU:0, one launch (start us, length us, event | category | flops | bytes accessed | tf_op | source)
XLA Modules:
  0.0 2316.4 jit_solution(14734667101272722325)
XLA Ops:
  34.2 12.0 all-gather
  51.0 8.5 all-gather.1
  64.3 10.5 all-gather.3
  74.9 7.8 fusion.231
  82.7 8.5 all-gather.6
  91.9 9.2 all-gather.9
  105.8 11.3 all-gather.10
  121.9 9.2 all-gather.12
  131.1 7.8 fusion.224
  140.5 14.0 all-reduce
  166.4 10.5 collective-permute-start
  190.0 8.8 collective-permute-start.3
  198.8 30.9 %collective-permute-done.23 = s32[256]{0:T(256)S(1)} collective-permute-done((s32[256]{0:T(256)S(1)}, s32[256]{0:T(256)S(1)}, u32[]{:S(2)}, u32[]{:S(2)}) %collective-permute-start.23) | collective-permute-done | bytes 1056 | tf_op jit(solution)/shard_map/ppermute | solution.py:18
  229.7 8.7 collective-permute-start.4
  238.5 32.8 %collective-permute-start.5 = (bf16[256,1536]{1,0:T(8,128)(2,1)S(1)}, bf16[256,1536]{1,0:T(8,128)(2,1)S(1)}, u32[]{:S(2)}, u32[]{:S(2)}) collective-permute-start(bf16[256,1536]{1,0:T(8,128)(2,1)S(1)} %pad_maximum_fusion.4), channel_id=1, source_target_pairs={{0,1},{1,2},{2,3},{3,4},{4,5},{5,6},{6,7},{7,8},{8,9},{9,10},{10,1... | collective-permute-start | bytes 2359304 | tf_op jit(solution)/shard_map/ppermute | solution.py:18
  292.3 18.6 collective-permute-done.6
  313.2 66.3 %collective-permute-done.7 = bf16[256,1536]{1,0:T(8,128)(2,1)S(1)} collective-permute-done((bf16[256,1536]{1,0:T(8,128)(2,1)S(1)}, bf16[256,1536]{1,0:T(8,128)(2,1)S(1)}, u32[]{:S(2)}, u32[]{:S(2)}) %collective-permute-start.7) | collective-permute-done | bytes 786464 | tf_op jit(solution)/shard_map/ppermute | solution.py:18
  383.3 12.7 collective-permute-done.11
  396.9 8.5 fusion.258
  405.4 7.8 copy.58
  413.1 7.8 copy.60
  421.0 46.2 %while.56 = (s32[]{:T(128)}, bf16[6,256,2,64]{1,3,2,0:T(8,128)(2,1)S(1)}, f32[6,2,256]{2,1,0:T(2,128)S(1)}, bf16[6,3328,2,64]{1,3,2,0:T(8,128)(2,1)}, bf16[6,256...) while((s32[]{:T(128)}, ...), condition=%wide.region_5.6_spmd.clone, body=%wide.region_2.5_spmd.clone.sunk | while | flops 451542528 | bytes 24085872 | solution.py:158
  469.6 11.4 fusion.130
  489.2 17.5 collective-permute-start.24
  506.7 14.5 collective-permute-start.25
  529.0 50.0 %all-gather.15 = bf16[1,3072]{1,0:T(2,128)(2,1)S(1)} all-gather(bf16[1,384]{1,0:T(2,128)(2,1)S(1)} %get-tuple-element.563), channel_id=17, replica_groups=mesh['group'=8,'rep'=4] {'group'}, dimensions={1}, use_global_device_ids=true | all-gather | bytes 6912 | tf_op jit(solution)/shard_map/all_gather | solution.py:106
  601.5 13.5 collective-permute-done.29
  618.3 8.3 collective-permute-done.30
  628.8 84.9 %collective-permute-done.31 = bf16[256,1536]{1,0:T(8,128)(2,1)S(1)} collective-permute-done((bf16[256,1536]{1,0:T(8,128)(2,1)S(1)}, bf16[256,1536]{1,0:T(8,128)(2,1)S(1)}, u32[]{:S(2)}, u32[]{:S(2)}) %collective-permute-start.31) | collective-permute-done | bytes 786464 | tf_op jit(solution)/shard_map/ppermute | solution.py:18
  717.5 10.0 collective-permute-done.35
  728.4 8.4 fusion.257
  736.8 7.8 copy.64
  744.6 7.7 copy.66
  752.4 46.2 %while.57 = (s32[]{:T(128)}, bf16[6,256,2,64]{1,3,2,0:T(8,128)(2,1)S(1)}, f32[6,2,256]{2,1,0:T(2,128)S(1)}, bf16[6,3328,2,64]{1,3,2,0:T(8,128)(2,1)}, bf16[6,256...) while((s32[]{:T(128)}, ...), condition=%wide.region_13.14_spmd.clone, body=%wide.region_10.13_spmd.clone.sunk | while | flops 451542528 | bytes 24085872 | solution.py:158
  800.8 11.1 fusion.133
  833.7 121.5 %while.58 = (s32[]{:T(128)}, f32[6,256,2,64]{1,3,2,0:T(8,128)}, f32[6,3328,2,64]{1,3,2,0:T(8,128)}, f32[6,3328,2,64]{1,3,2,0:T(8,128)}, bf16[6,3328,2,64]{1,3,2,...) while((s32[]{:T(128)}, f32[6,256,2,64]{1,3,2,0:T(8,128)}, ...), condition=%wide.region_20.21_spmd.clone, body=%wide.region_18.20_spmd.clone.sunk | while | flops 1107557888 | bytes 75987424 | solution.py:259
  955.2 10.0 fusion.91
  974.7 27.5 %collective-permute-start.39 = (bf16[256,1536]{0,1:T(8,128)(2,1)S(1)}, bf16[256,1536]{0,1:T(8,128)(2,1)S(1)}, u32[]{:S(2)}, u32[]{:S(2)}) collective-permute-start(bf16[256,1536]{0,1:T(8,128)(2,1)S(1)} %get-tuple-element.538), channel_id=1, source_target_pairs={{0,2},{1,3},{2,4},{3,5},{4,6},{5,7},{6,8},{7,9},{8,10},{9,11},{10,... | collective-permute-start | bytes 2359304 | tf_op jit(solution)/shard_map/ppermute | solution.py:18
  1003.5 12.2 collective-permute-start.41
  1017.0 66.7 %collective-permute-done.38 = bf16[256,1536]{0,1:T(8,128)(2,1)S(1)} collective-permute-done((bf16[256,1536]{0,1:T(8,128)(2,1)S(1)}, bf16[256,1536]{0,1:T(8,128)(2,1)S(1)}, u32[]{:S(2)}, u32[]{:S(2)}) %collective-permute-start.38) | collective-permute-done | bytes 786464 | tf_op jit(solution)/shard_map/ppermute | solution.py:18
  1100.7 48.4 %collective-permute-start.47 = (bf16[256,1536]{0,1:T(8,128)(2,1)S(1)}, bf16[256,1536]{0,1:T(8,128)(2,1)}, u32[]{:S(2)}, u32[]{:S(2)}) collective-permute-start(bf16[256,1536]{0,1:T(8,128)(2,1)S(1)} %get-tuple-element.530), channel_id=1, source_target_pairs={{0,6},{1,7},{2,8},{3,9},{4,10},{5,11},{6,12},{7,13},{8,14},{9,15},... | collective-permute-start | bytes 2359304 | tf_op jit(solution)/shard_map/ppermute | solution.py:18
  1152.7 35.9 %collective-permute-done.46 = bf16[256,1536]{0,1:T(8,128)(2,1)} collective-permute-done((bf16[256,1536]{0,1:T(8,128)(2,1)}, bf16[256,1536]{0,1:T(8,128)(2,1)}, u32[]{:S(2)}, u32[]{:S(2)}) %collective-permute-start.46) | collective-permute-done | bytes 786464 | tf_op jit(solution)/shard_map/ppermute | solution.py:18
  1219.3 126.5 %while.59 = (s32[]{:T(128)}, f32[6,256,2,64]{1,3,2,0:T(8,128)}, f32[6,3328,2,64]{1,3,2,0:T(8,128)}, f32[6,3328,2,64]{1,3,2,0:T(8,128)}, bf16[6,3328,2,64]{1,3,2,...) while((s32[]{:T(128)}, f32[6,256,2,64]{1,3,2,0:T(8,128)}, ...), condition=%wide.region_27.28_spmd.clone, body=%wide.region_25.27_spmd.clone.sunk | while | flops 1107557888 | bytes 75987424 | solution.py:259
  1350.3 16.8 fusion.90
  1372.8 8.7 collective-permute-start.49
  1382.8 23.1 collective-permute-start.51
  1407.3 12.2 collective-permute-start.53
  1420.8 66.4 %collective-permute-done.50 = bf16[256,1536]{0,1:T(8,128)(2,1)S(1)} collective-permute-done((bf16[256,1536]{0,1:T(8,128)(2,1)S(1)}, bf16[256,1536]{0,1:T(8,128)(2,1)S(1)}, u32[]{:S(2)}, u32[]{:S(2)}) %collective-permute-start.50) | collective-permute-done | bytes 786464 | tf_op jit(solution)/shard_map/ppermute | solution.py:18
  1495.6 15.5 collective-permute-start.57
  1512.4 49.2 %collective-permute-start.59 = (bf16[256,1536]{0,1:T(8,128)(2,1)S(1)}, bf16[256,1536]{0,1:T(8,128)(2,1)S(1)}, u32[]{:S(2)}, u32[]{:S(2)}) collective-permute-start(bf16[256,1536]{0,1:T(8,128)(2,1)S(1)} %get-tuple-element.518), channel_id=1, source_target_pairs={{0,6},{1,7},{2,8},{3,9},{4,10},{5,11},{6,12},{7,13},{8,14},{9,15},... | collective-permute-start | bytes 2359304 | tf_op jit(solution)/shard_map/ppermute | solution.py:18
  1563.0 20.7 collective-permute-done.58
  1630.0 85.8 %reduce-scatter.27.cloned.1.call-done = bf16[96,2304]{1,0:T(8,128)(2,1)} async-done(((bf16[768,2304]{1,0:T(8,128)(2,1)}), bf16[96,2304]{1,0:T(8,128)(2,1)}) %reduce-scatter.27.cloned.1.call-update) | async-done | bytes 442384 | tf_op jit(solution)/shard_map/reduce_scatter | solution.py:309
  1715.8 57.2 %reduce-scatter.37.cloned.1.call-done = bf16[96,3072]{1,0:T(8,128)(2,1)} async-done(((bf16[768,3072]{1,0:T(8,128)(2,1)}), bf16[96,3072]{1,0:T(8,128)(2,1)}) %reduce-scatter.37.cloned.1.call-update) | async-done | bytes 589840 | tf_op jit(solution)/shard_map/reduce_scatter | solution.py:318
  1773.0 57.1 %reduce-scatter.41.cloned.1.call-done = bf16[384,768]{1,0:T(8,128)(2,1)} async-done(((bf16[3072,768]{1,0:T(8,128)(2,1)}), bf16[384,768]{1,0:T(8,128)(2,1)}) %reduce-scatter.41.cloned.1.call-update) | async-done | bytes 589840 | tf_op jit(solution)/shard_map/reduce_scatter | solution.py:324
  1830.2 57.1 %reduce-scatter.39.cloned.1.call-done = bf16[384,768]{1,0:T(8,128)(2,1)} async-done(((bf16[3072,768]{1,0:T(8,128)(2,1)}), bf16[384,768]{1,0:T(8,128)(2,1)}) %reduce-scatter.39.cloned.1.call-update) | async-done | bytes 589840 | tf_op jit(solution)/shard_map/reduce_scatter | solution.py:324
  1887.3 57.1 %reduce-scatter.35.cloned.1.call-done = bf16[96,3072]{1,0:T(8,128)(2,1)} async-done(((bf16[768,3072]{1,0:T(8,128)(2,1)}), bf16[96,3072]{1,0:T(8,128)(2,1)}) %reduce-scatter.35.cloned.1.call-update) | async-done | bytes 589840 | tf_op jit(solution)/shard_map/reduce_scatter | solution.py:318
  1946.0 22.9 all-reduce.6
  1981.8 36.3 %reduce-scatter.49.cloned.1.call-done = bf16[96,2]{1,0:T(8,128)(2,1)} async-done(((bf16[768,2]{1,0:T(8,128)(2,1)}), bf16[96,2]{1,0:T(8,128)(2,1)}) %reduce-scatter.49.cloned.1.call-update) | async-done | bytes 400
  2018.9 36.5 %reduce-scatter.45.cloned.1.call-done = bf16[96,3]{1,0:T(8,128)(2,1)} async-done(((bf16[768,3]{1,0:T(8,128)(2,1)}), bf16[96,3]{1,0:T(8,128)(2,1)}) %reduce-scatter.45.cloned.1.call-update) | async-done | bytes 592
  2057.4 34.5 %reduce-scatter.51.cloned.1.call-done = bf16[96,2]{1,0:T(8,128)(2,1)} async-done(((bf16[768,2]{1,0:T(8,128)(2,1)}), bf16[96,2]{1,0:T(8,128)(2,1)}) %reduce-scatter.51.cloned.1.call-update) | async-done | bytes 400
  2092.7 35.9 %reduce-scatter.47.cloned.1.call-done = bf16[96,2]{1,0:T(8,128)(2,1)} async-done(((bf16[768,2]{1,0:T(8,128)(2,1)}), bf16[96,2]{1,0:T(8,128)(2,1)}) %reduce-scatter.47.cloned.1.call-update) | async-done | bytes 400
  2129.5 36.5 %reduce-scatter.43.cloned.1.call-done = bf16[96,3]{1,0:T(8,128)(2,1)} async-done(((bf16[768,3]{1,0:T(8,128)(2,1)}), bf16[96,3]{1,0:T(8,128)(2,1)}) %reduce-scatter.43.cloned.1.call-update) | async-done | bytes 592
  2166.8 11.9 all-reduce.7
  2181.6 121.3 %all-reduce.11.cloned.1.call-done = (bf16[1,96,2304]{2,1,0:T(8,128)(2,1)}, bf16[1,96,2304]{2,1,0:T(8,128)(2,1)}, bf16[1,96,768]{2,1,0:T(8,128)(2,1)}, bf16[1,96,...) async-done(((bf16[1,96,2304]{2,1,0:T(8,128)(2,1)}, ...) | async-done | bytes 3538960 | tf_op jit(solution)/shard_map/psum | solution.py:338
  (801 shorter events, 676.3 us)
Async XLA Ops:
  7.2 155.8 %all-gather.27.cloned.1.call-start = ((), (), s32[]{:S(2)}) async-start(), calls=%async_computation.22 | async-start | bytes 3981312 | tf_op jit(solution)/shard_map/all_gather | solution.py:102
  9.5 457.7 %all-gather.29.cloned.1.call-start = ((), (), s32[]{:S(2)}) async-start(), calls=%async_computation.23 | async-start | bytes 1327104 | tf_op jit(solution)/shard_map/all_gather | solution.py:104
  11.3 458.3 %all-gather.31.cloned.1.call-start = ((), (), s32[]{:S(2)}) async-start(), calls=%async_computation.24 | async-start | bytes 5308416 | tf_op jit(solution)/shard_map/all_gather | solution.py:105
  12.5 468.6 %all-gather.33.cloned.1.call-start = ((), (), s32[]{:S(2)}) async-start(), calls=%async_computation.25 | async-start | bytes 5308416 | tf_op jit(solution)/shard_map/all_gather | solution.py:107
  13.7 472.0 %all-gather.35.cloned.1.call-start = ((), (), s32[]{:S(2)}) async-start(), calls=%async_computation.26 | async-start | bytes 3981312 | tf_op jit(solution)/shard_map/all_gather | solution.py:102
  14.3 784.3 %all-gather.37.cloned.1.call-start = ((), (), s32[]{:S(2)}) async-start(), calls=%async_computation.27 | async-start | bytes 1327104 | tf_op jit(solution)/shard_map/all_gather | solution.py:104
  14.9 785.9 %all-gather.39.cloned.1.call-start = ((), (), s32[]{:S(2)}) async-start(), calls=%async_computation.28 | async-start | bytes 5308416 | tf_op jit(solution)/shard_map/all_gather | solution.py:105
  14.9 139.6 %collective-permute-start.12 = (s32[256]{0:T(256)S(1)}, s32[256]{0:T(256)S(1)}, u32[]{:S(2)}, u32[]{:S(2)}) collective-permute-start(s32[256]{0:T(256)S(1)} %broadcast_add_fusion), channel_id=1, source_target_pairs={{0,6},{1,7},{2,8},{3,9},{4,10},{5,11},{6,12},{7,13},{8,14},{9,15},... | collective-permute-start | bytes 3080 | tf_op jit(solution)/shard_map/ppermute | solution.py:18
  20.4 137.1 %collective-permute-start.13 = (s32[256]{0:T(256)S(1)}, s32[256]{0:T(256)S(1)}, u32[]{:S(2)}, u32[]{:S(2)}) collective-permute-start(s32[256]{0:T(256)S(1)} %broadcast_add_fusion), channel_id=1, source_target_pairs={{0,5},{1,6},{2,7},{3,8},{4,9},{5,10},{6,11},{7,12},{8,13},{9,14},{... | collective-permute-start | bytes 3080 | tf_op jit(solution)/shard_map/ppermute | solution.py:18
  25.0 133.7 %collective-permute-start.14 = (s32[256]{0:T(256)S(1)}, s32[256]{0:T(256)S(1)}, u32[]{:S(2)}, u32[]{:S(2)}) collective-permute-start(s32[256]{0:T(256)S(1)} %broadcast_add_fusion), channel_id=1, source_target_pairs={{0,4},{1,5},{2,6},{3,7},{4,8},{5,9},{6,10},{7,11},{8,12},{9,13},{1... | collective-permute-start | bytes 3080 | tf_op jit(solution)/shard_map/ppermute | solution.py:18
  26.8 133.3 %collective-permute-start.15 = (s32[256]{0:T(256)S(1)}, s32[256]{0:T(256)S(1)}, u32[]{:S(2)}, u32[]{:S(2)}) collective-permute-start(s32[256]{0:T(256)S(1)} %broadcast_add_fusion), channel_id=1, source_target_pairs={{0,3},{1,4},{2,5},{3,6},{4,7},{5,8},{6,9},{7,10},{8,11},{9,12},{10... | collective-permute-start | bytes 3080 | tf_op jit(solution)/shard_map/ppermute | solution.py:18
  32.2 129.3 %collective-permute-start.16 = (s32[256]{0:T(256)S(1)}, s32[256]{0:T(256)S(1)}, u32[]{:S(2)}, u32[]{:S(2)}) collective-permute-start(s32[256]{0:T(256)S(1)} %broadcast_add_fusion), channel_id=1, source_target_pairs={{0,2},{1,3},{2,4},{3,5},{4,6},{5,7},{6,8},{7,9},{8,10},{9,11},{10,... | collective-permute-start | bytes 3080 | tf_op jit(solution)/shard_map/ppermute | solution.py:18
  33.5 778.4 %all-gather.41.cloned.1.call-start = ((), (), s32[]{:S(2)}) async-start(), calls=%async_computation.29 | async-start | bytes 5308416 | tf_op jit(solution)/shard_map/all_gather | solution.py:107
  166.4 72.1 %collective-permute-start = (bf16[256,1536]{1,0:T(8,128)(2,1)S(1)}, bf16[256,1536]{1,0:T(8,128)(2,1)}, u32[]{:S(2)}, u32[]{:S(2)}) collective-permute-start(bf16[256,1536]{1,0:T(8,128)(2,1)S(1)} %pad_maximum_fusion.4), channel_id=1, source_target_pairs={{0,6},{1,7},{2,8},{3,9},{4,10},{5,11},{6,12},{7,13},{8,14},{9,15},... | collective-permute-start | bytes 2359304 | tf_op jit(solution)/shard_map/ppermute | solution.py:18
  178.3 95.1 %collective-permute-start.1 = (bf16[256,1536]{1,0:T(8,128)(2,1)S(1)}, bf16[256,1536]{1,0:T(8,128)(2,1)}, u32[]{:S(2)}, u32[]{:S(2)}) collective-permute-start(bf16[256,1536]{1,0:T(8,128)(2,1)S(1)} %pad_maximum_fusion.4), channel_id=1, source_target_pairs={{0,5},{1,6},{2,7},{3,8},{4,9},{5,10},{6,11},{7,12},{8,13},{9,14},{... | collective-permute-start | bytes 2359304 | tf_op jit(solution)/shard_map/ppermute | solution.py:18
  186.7 90.1 %collective-permute-start.2 = (bf16[256,1536]{1,0:T(8,128)(2,1)S(1)}, bf16[256,1536]{1,0:T(8,128)(2,1)}, u32[]{:S(2)}, u32[]{:S(2)}) collective-permute-start(bf16[256,1536]{1,0:T(8,128)(2,1)S(1)} %pad_maximum_fusion.4), channel_id=1, source_target_pairs={{0,4},{1,5},{2,6},{3,7},{4,8},{5,9},{6,10},{7,11},{8,12},{9,13},{1... | collective-permute-start | bytes 2359304 | tf_op jit(solution)/shard_map/ppermute | solution.py:18
  190.0 90.2 %collective-permute-start.3 = (bf16[256,1536]{1,0:T(8,128)(2,1)S(1)}, bf16[256,1536]{1,0:T(8,128)(2,1)}, u32[]{:S(2)}, u32[]{:S(2)}) collective-permute-start(bf16[256,1536]{1,0:T(8,128)(2,1)S(1)} %pad_maximum_fusion.4), channel_id=1, source_target_pairs={{0,3},{1,4},{2,5},{3,6},{4,7},{5,8},{6,9},{7,10},{8,11},{9,12},{10... | collective-permute-start | bytes 2359304 | tf_op jit(solution)/shard_map/ppermute | solution.py:18
  276.8 102.6 %collective-permute-start.7 = (bf16[256,1536]{1,0:T(8,128)(2,1)S(1)}, bf16[256,1536]{1,0:T(8,128)(2,1)S(1)}, u32[]{:S(2)}, u32[]{:S(2)}) collective-permute-start(bf16[256,1536]{1,0:T(8,128)(2,1)S(1)} %pad_maximum_fusion.4), channel_id=1, source_target_pairs={{2,0},{3,1},{4,2},{5,3},{6,4},{7,5},{8,6},{9,7},{10,8},{11,9},{12,... | collective-permute-start | bytes 2359304 | tf_op jit(solution)/shard_map/ppermute | solution.py:18
  280.2 100.2 %collective-permute-start.8 = (bf16[256,1536]{1,0:T(8,128)(2,1)S(1)}, bf16[256,1536]{1,0:T(8,128)(2,1)S(1)}, u32[]{:S(2)}, u32[]{:S(2)}) collective-permute-start(bf16[256,1536]{1,0:T(8,128)(2,1)S(1)} %pad_maximum_fusion.4), channel_id=1, source_target_pairs={{3,0},{4,1},{5,2},{6,3},{7,4},{8,5},{9,6},{10,7},{11,8},{12,9},{13... | collective-permute-start | bytes 2359304 | tf_op jit(solution)/shard_map/ppermute | solution.py:18
  283.6 97.8 %collective-permute-start.9 = (bf16[256,1536]{1,0:T(8,128)(2,1)S(1)}, bf16[256,1536]{1,0:T(8,128)(2,1)S(1)}, u32[]{:S(2)}, u32[]{:S(2)}) collective-permute-start(bf16[256,1536]{1,0:T(8,128)(2,1)S(1)} %pad_maximum_fusion.4), channel_id=1, source_target_pairs={{4,0},{5,1},{6,2},{7,3},{8,4},{9,5},{10,6},{11,7},{12,8},{13,9},{1... | collective-permute-start | bytes 2359304 | tf_op jit(solution)/shard_map/ppermute | solution.py:18
  289.2 93.1 %collective-permute-start.10 = (bf16[256,1536]{1,0:T(8,128)(2,1)S(1)}, bf16[256,1536]{1,0:T(8,128)(2,1)S(1)}, u32[]{:S(2)}, u32[]{:S(2)}) collective-permute-start(bf16[256,1536]{1,0:T(8,128)(2,1)S(1)} %pad_maximum_fusion.4), channel_id=1, source_target_pairs={{5,0},{6,1},{7,2},{8,3},{9,4},{10,5},{11,6},{12,7},{13,8},{14,9},{... | collective-permute-start | bytes 2359304 | tf_op jit(solution)/shard_map/ppermute | solution.py:18
  310.9 85.0 %collective-permute-start.11 = (bf16[256,1536]{1,0:T(8,128)(2,1)S(1)}, bf16[256,1536]{1,0:T(8,128)(2,1)S(1)}, u32[]{:S(2)}, u32[]{:S(2)}) collective-permute-start(bf16[256,1536]{1,0:T(8,128)(2,1)S(1)} %pad_maximum_fusion.4), channel_id=1, source_target_pairs={{6,0},{7,1},{8,2},{9,3},{10,4},{11,5},{12,6},{13,7},{14,8},{15,9},... | collective-permute-start | bytes 2359304 | tf_op jit(solution)/shard_map/ppermute | solution.py:18
  489.2 92.2 %collective-permute-start.24 = (bf16[256,1536]{1,0:T(8,128)(2,1)S(1)}, bf16[256,1536]{1,0:T(8,128)(2,1)}, u32[]{:S(2)}, u32[]{:S(2)}) collective-permute-start(bf16[256,1536]{1,0:T(8,128)(2,1)S(1)} %pad_maximum_fusion.5), channel_id=1, source_target_pairs={{0,6},{1,7},{2,8},{3,9},{4,10},{5,11},{6,12},{7,13},{8,14},{9,15},... | collective-permute-start | bytes 2359304 | tf_op jit(solution)/shard_map/ppermute | solution.py:18
  506.7 78.1 %collective-permute-start.25 = (bf16[256,1536]{1,0:T(8,128)(2,1)S(1)}, bf16[256,1536]{1,0:T(8,128)(2,1)}, u32[]{:S(2)}, u32[]{:S(2)}) collective-permute-start(bf16[256,1536]{1,0:T(8,128)(2,1)S(1)} %pad_maximum_fusion.5), channel_id=1, source_target_pairs={{0,5},{1,6},{2,7},{3,8},{4,9},{5,10},{6,11},{7,12},{8,13},{9,14},{... | collective-permute-start | bytes 2359304 | tf_op jit(solution)/shard_map/ppermute | solution.py:18
  521.2 67.0 %collective-permute-start.26 = (bf16[256,1536]{1,0:T(8,128)(2,1)S(1)}, bf16[256,1536]{1,0:T(8,128)(2,1)}, u32[]{:S(2)}, u32[]{:S(2)}) collective-permute-start(bf16[256,1536]{1,0:T(8,128)(2,1)S(1)} %pad_maximum_fusion.5), channel_id=1, source_target_pairs={{0,4},{1,5},{2,6},{3,7},{4,8},{5,9},{6,10},{7,11},{8,12},{9,13},{1... | collective-permute-start | bytes 2359304 | tf_op jit(solution)/shard_map/ppermute | solution.py:18
  523.4 68.3 %collective-permute-start.27 = (bf16[256,1536]{1,0:T(8,128)(2,1)S(1)}, bf16[256,1536]{1,0:T(8,128)(2,1)}, u32[]{:S(2)}, u32[]{:S(2)}) collective-permute-start(bf16[256,1536]{1,0:T(8,128)(2,1)S(1)} %pad_maximum_fusion.5), channel_id=1, source_target_pairs={{0,3},{1,4},{2,5},{3,6},{4,7},{5,8},{6,9},{7,10},{8,11},{9,12},{10... | collective-permute-start | bytes 2359304 | tf_op jit(solution)/shard_map/ppermute | solution.py:18
  529.0 1101.0 %reduce-scatter.33.cloned.1.call-start = ((), (), s32[]{:S(2)}) async-start(), calls=%async_computation.17 | async-start | bytes 1327104 | tf_op jit(solution)/shard_map/reduce_scatter | solution.py:315
  588.2 125.5 %collective-permute-start.31 = (bf16[256,1536]{1,0:T(8,128)(2,1)S(1)}, bf16[256,1536]{1,0:T(8,128)(2,1)S(1)}, u32[]{:S(2)}, u32[]{:S(2)}) collective-permute-start(bf16[256,1536]{1,0:T(8,128)(2,1)S(1)} %pad_maximum_fusion.5), channel_id=1, source_target_pairs={{2,0},{3,1},{4,2},{5,3},{6,4},{7,5},{8,6},{9,7},{10,8},{11,9},{12,... | collective-permute-start | bytes 2359304 | tf_op jit(solution)/shard_map/ppermute | solution.py:18
  591.6 123.0 %collective-permute-start.32 = (bf16[256,1536]{1,0:T(8,128)(2,1)S(1)}, bf16[256,1536]{1,0:T(8,128)(2,1)S(1)}, u32[]{:S(2)}, u32[]{:S(2)}) collective-permute-start(bf16[256,1536]{1,0:T(8,128)(2,1)S(1)} %pad_maximum_fusion.5), channel_id=1, source_target_pairs={{3,0},{4,1},{5,2},{6,3},{7,4},{8,5},{9,6},{10,7},{11,8},{12,9},{13... | collective-permute-start | bytes 2359304 | tf_op jit(solution)/shard_map/ppermute | solution.py:18
  598.2 117.4 %collective-permute-start.33 = (bf16[256,1536]{1,0:T(8,128)(2,1)S(1)}, bf16[256,1536]{1,0:T(8,128)(2,1)S(1)}, u32[]{:S(2)}, u32[]{:S(2)}) collective-permute-start(bf16[256,1536]{1,0:T(8,128)(2,1)S(1)} %pad_maximum_fusion.5), channel_id=1, source_target_pairs={{4,0},{5,1},{6,2},{7,3},{8,4},{9,5},{10,6},{11,7},{12,8},{13,9},{1... | collective-permute-start | bytes 2359304 | tf_op jit(solution)/shard_map/ppermute | solution.py:18
  615.0 101.5 %collective-permute-start.34 = (bf16[256,1536]{1,0:T(8,128)(2,1)S(1)}, bf16[256,1536]{1,0:T(8,128)(2,1)S(1)}, u32[]{:S(2)}, u32[]{:S(2)}) collective-permute-start(bf16[256,1536]{1,0:T(8,128)(2,1)S(1)} %pad_maximum_fusion.5), channel_id=1, source_target_pairs={{5,0},{6,1},{7,2},{8,3},{9,4},{10,5},{11,6},{12,7},{13,8},{14,9},{... | collective-permute-start | bytes 2359304 | tf_op jit(solution)/shard_map/ppermute | solution.py:18
  626.6 100.9 %collective-permute-start.35 = (bf16[256,1536]{1,0:T(8,128)(2,1)S(1)}, bf16[256,1536]{1,0:T(8,128)(2,1)S(1)}, u32[]{:S(2)}, u32[]{:S(2)}) collective-permute-start(bf16[256,1536]{1,0:T(8,128)(2,1)S(1)} %pad_maximum_fusion.5), channel_id=1, source_target_pairs={{6,0},{7,1},{8,2},{9,3},{10,4},{11,5},{12,6},{13,7},{14,8},{15,9},... | collective-permute-start | bytes 2359304 | tf_op jit(solution)/shard_map/ppermute | solution.py:18
  973.4 110.3 %collective-permute-start.38 = (bf16[256,1536]{0,1:T(8,128)(2,1)S(1)}, bf16[256,1536]{0,1:T(8,128)(2,1)S(1)}, u32[]{:S(2)}, u32[]{:S(2)}) collective-permute-start(bf16[256,1536]{0,1:T(8,128)(2,1)S(1)} %get-tuple-element.539), channel_id=1, source_target_pairs={{2,0},{3,1},{4,2},{5,3},{6,4},{7,5},{8,6},{9,7},{10,8},{11,9},{12,... | collective-permute-start | bytes 2359304 | tf_op jit(solution)/shard_map/ppermute | solution.py:18
  974.7 116.4 %collective-permute-start.39 = (bf16[256,1536]{0,1:T(8,128)(2,1)S(1)}, bf16[256,1536]{0,1:T(8,128)(2,1)S(1)}, u32[]{:S(2)}, u32[]{:S(2)}) collective-permute-start(bf16[256,1536]{0,1:T(8,128)(2,1)S(1)} %get-tuple-element.538), channel_id=1, source_target_pairs={{0,2},{1,3},{2,4},{3,5},{4,6},{5,7},{6,8},{7,9},{8,10},{9,11},{10,... | collective-permute-start | bytes 2359304 | tf_op jit(solution)/shard_map/ppermute | solution.py:18
  1002.2 90.2 %collective-permute-start.40 = (bf16[256,1536]{0,1:T(8,128)(2,1)S(1)}, bf16[256,1536]{0,1:T(8,128)(2,1)S(1)}, u32[]{:S(2)}, u32[]{:S(2)}) collective-permute-start(bf16[256,1536]{0,1:T(8,128)(2,1)S(1)} %get-tuple-element.537), channel_id=1, source_target_pairs={{3,0},{4,1},{5,2},{6,3},{7,4},{8,5},{9,6},{10,7},{11,8},{12,9},{13... | collective-permute-start | bytes 2359304 | tf_op jit(solution)/shard_map/ppermute | solution.py:18
  1003.5 95.8 %collective-permute-start.41 = (bf16[256,1536]{0,1:T(8,128)(2,1)S(1)}, bf16[256,1536]{0,1:T(8,128)(2,1)S(1)}, u32[]{:S(2)}, u32[]{:S(2)}) collective-permute-start(bf16[256,1536]{0,1:T(8,128)(2,1)S(1)} %get-tuple-element.536), channel_id=1, source_target_pairs={{0,3},{1,4},{2,5},{3,6},{4,7},{5,8},{6,9},{7,10},{8,11},{9,12},{10... | collective-permute-start | bytes 2359304 | tf_op jit(solution)/shard_map/ppermute | solution.py:18
  1015.7 84.9 %collective-permute-start.42 = (bf16[256,1536]{0,1:T(8,128)(2,1)S(1)}, bf16[256,1536]{0,1:T(8,128)(2,1)S(1)}, u32[]{:S(2)}, u32[]{:S(2)}) collective-permute-start(bf16[256,1536]{0,1:T(8,128)(2,1)S(1)} %get-tuple-element.535), channel_id=1, source_target_pairs={{4,0},{5,1},{6,2},{7,3},{8,4},{9,5},{10,6},{11,7},{12,8},{13,9},{1... | collective-permute-start | bytes 2359304 | tf_op jit(solution)/shard_map/ppermute | solution.py:18
  1083.7 69.0 %collective-permute-start.43 = (bf16[256,1536]{0,1:T(8,128)(2,1)}, bf16[256,1536]{0,1:T(8,128)(2,1)}, u32[]{:S(2)}, u32[]{:S(2)}) collective-permute-start(bf16[256,1536]{0,1:T(8,128)(2,1)} %get-tuple-element.534), channel_id=1, source_target_pairs={{0,4},{1,5},{2,6},{3,7},{4,8},{5,9},{6,10},{7,11},{8,12},{9,13},{1... | collective-permute-start | bytes 2359304 | tf_op jit(solution)/shard_map/ppermute | solution.py:18
  1099.4 89.2 %collective-permute-start.46 = (bf16[256,1536]{0,1:T(8,128)(2,1)}, bf16[256,1536]{0,1:T(8,128)(2,1)}, u32[]{:S(2)}, u32[]{:S(2)}) collective-permute-start(bf16[256,1536]{0,1:T(8,128)(2,1)} %get-tuple-element.531), channel_id=1, source_target_pairs={{6,0},{7,1},{8,2},{9,3},{10,4},{11,5},{12,6},{13,7},{14,8},{15,9},... | collective-permute-start | bytes 2359304 | tf_op jit(solution)/shard_map/ppermute | solution.py:18
  1100.7 87.9 %collective-permute-start.47 = (bf16[256,1536]{0,1:T(8,128)(2,1)S(1)}, bf16[256,1536]{0,1:T(8,128)(2,1)}, u32[]{:S(2)}, u32[]{:S(2)}) collective-permute-start(bf16[256,1536]{0,1:T(8,128)(2,1)S(1)} %get-tuple-element.530), channel_id=1, source_target_pairs={{0,6},{1,7},{2,8},{3,9},{4,10},{5,11},{6,12},{7,13},{8,14},{9,15},... | collective-permute-start | bytes 2359304 | tf_op jit(solution)/shard_map/ppermute | solution.py:18
  1150.7 479.3 %reduce-scatter.31.cloned.1.call-start = ((), (), s32[]{:S(2)}) async-start(), calls=%async_computation.16 | async-start | bytes 1327104 | tf_op jit(solution)/shard_map/reduce_scatter | solution.py:315
  1208.7 421.3 %reduce-scatter.29.cloned.1.call-start = ((), (), s32[]{:S(2)}) async-start(), calls=%async_computation.15 | async-start | bytes 3981312 | tf_op jit(solution)/shard_map/reduce_scatter | solution.py:309
  1350.2 365.6 %reduce-scatter.27.cloned.1.call-start = ((), (), s32[]{:S(2)}) async-start(), calls=%async_computation.14 | async-start | bytes 3981312 | tf_op jit(solution)/shard_map/reduce_scatter | solution.py:309
  1381.5 105.7 %collective-permute-start.50 = (bf16[256,1536]{0,1:T(8,128)(2,1)S(1)}, bf16[256,1536]{0,1:T(8,128)(2,1)S(1)}, u32[]{:S(2)}, u32[]{:S(2)}) collective-permute-start(bf16[256,1536]{0,1:T(8,128)(2,1)S(1)} %get-tuple-element.527), channel_id=1, source_target_pairs={{2,0},{3,1},{4,2},{5,3},{6,4},{7,5},{8,6},{9,7},{10,8},{11,9},{12,... | collective-permute-start | bytes 2359304 | tf_op jit(solution)/shard_map/ppermute | solution.py:18
  1382.8 111.4 %collective-permute-start.51 = (bf16[256,1536]{0,1:T(8,128)(2,1)S(1)}, bf16[256,1536]{0,1:T(8,128)(2,1)S(1)}, u32[]{:S(2)}, u32[]{:S(2)}) collective-permute-start(bf16[256,1536]{0,1:T(8,128)(2,1)S(1)} %get-tuple-element.526), channel_id=1, source_target_pairs={{0,2},{1,3},{2,4},{3,5},{4,6},{5,7},{6,8},{7,9},{8,10},{9,11},{10,... | collective-permute-start | bytes 2359304 | tf_op jit(solution)/shard_map/ppermute | solution.py:18
  1406.0 89.6 %collective-permute-start.52 = (bf16[256,1536]{0,1:T(8,128)(2,1)S(1)}, bf16[256,1536]{0,1:T(8,128)(2,1)S(1)}, u32[]{:S(2)}, u32[]{:S(2)}) collective-permute-start(bf16[256,1536]{0,1:T(8,128)(2,1)S(1)} %get-tuple-element.525), channel_id=1, source_target_pairs={{3,0},{4,1},{5,2},{6,3},{7,4},{8,5},{9,6},{10,7},{11,8},{12,9},{13... | collective-permute-start | bytes 2359304 | tf_op jit(solution)/shard_map/ppermute | solution.py:18
  1407.3 103.8 %collective-permute-start.53 = (bf16[256,1536]{0,1:T(8,128)(2,1)S(1)}, bf16[256,1536]{0,1:T(8,128)(2,1)S(1)}, u32[]{:S(2)}, u32[]{:S(2)}) collective-permute-start(bf16[256,1536]{0,1:T(8,128)(2,1)S(1)} %get-tuple-element.524), channel_id=1, source_target_pairs={{0,3},{1,4},{2,5},{3,6},{4,7},{5,8},{6,9},{7,10},{8,11},{9,12},{10... | collective-permute-start | bytes 2359304 | tf_op jit(solution)/shard_map/ppermute | solution.py:18
  1419.5 92.9 %collective-permute-start.54 = (bf16[256,1536]{0,1:T(8,128)(2,1)S(1)}, bf16[256,1536]{0,1:T(8,128)(2,1)S(1)}, u32[]{:S(2)}, u32[]{:S(2)}) collective-permute-start(bf16[256,1536]{0,1:T(8,128)(2,1)S(1)} %get-tuple-element.523), channel_id=1, source_target_pairs={{4,0},{5,1},{6,2},{7,3},{8,4},{9,5},{10,6},{11,7},{12,8},{13,9},{1... | collective-permute-start | bytes 2359304 | tf_op jit(solution)/shard_map/ppermute | solution.py:18
  1487.2 75.8 %collective-permute-start.55 = (bf16[256,1536]{0,1:T(8,128)(2,1)S(1)}, bf16[256,1536]{0,1:T(8,128)(2,1)S(1)}, u32[]{:S(2)}, u32[]{:S(2)}) collective-permute-start(bf16[256,1536]{0,1:T(8,128)(2,1)S(1)} %get-tuple-element.522), channel_id=1, source_target_pairs={{0,4},{1,5},{2,6},{3,7},{4,8},{5,9},{6,10},{7,11},{8,12},{9,13},{1... | collective-permute-start | bytes 2359304 | tf_op jit(solution)/shard_map/ppermute | solution.py:18
  1494.3 68.7 %collective-permute-start.56 = (bf16[256,1536]{0,1:T(8,128)(2,1)S(1)}, bf16[256,1536]{0,1:T(8,128)(2,1)S(1)}, u32[]{:S(2)}, u32[]{:S(2)}) collective-permute-start(bf16[256,1536]{0,1:T(8,128)(2,1)S(1)} %get-tuple-element.521), channel_id=1, source_target_pairs={{5,0},{6,1},{7,2},{8,3},{9,4},{10,5},{11,6},{12,7},{13,8},{14,9},{... | collective-permute-start | bytes 2359304 | tf_op jit(solution)/shard_map/ppermute | solution.py:18
  1495.6 67.4 %collective-permute-start.57 = (bf16[256,1536]{0,1:T(8,128)(2,1)S(1)}, bf16[256,1536]{0,1:T(8,128)(2,1)S(1)}, u32[]{:S(2)}, u32[]{:S(2)}) collective-permute-start(bf16[256,1536]{0,1:T(8,128)(2,1)S(1)} %get-tuple-element.520), channel_id=1, source_target_pairs={{0,5},{1,6},{2,7},{3,8},{4,9},{5,10},{6,11},{7,12},{8,13},{9,14},{... | collective-permute-start | bytes 2359304 | tf_op jit(solution)/shard_map/ppermute | solution.py:18
  1511.1 72.6 %collective-permute-start.58 = (bf16[256,1536]{0,1:T(8,128)(2,1)S(1)}, bf16[256,1536]{0,1:T(8,128)(2,1)S(1)}, u32[]{:S(2)}, u32[]{:S(2)}) collective-permute-start(bf16[256,1536]{0,1:T(8,128)(2,1)S(1)} %get-tuple-element.519), channel_id=1, source_target_pairs={{6,0},{7,1},{8,2},{9,3},{10,4},{11,5},{12,6},{13,7},{14,8},{15,9},... | collective-permute-start | bytes 2359304 | tf_op jit(solution)/shard_map/ppermute | solution.py:18
  1512.4 71.4 %collective-permute-start.59 = (bf16[256,1536]{0,1:T(8,128)(2,1)S(1)}, bf16[256,1536]{0,1:T(8,128)(2,1)S(1)}, u32[]{:S(2)}, u32[]{:S(2)}) collective-permute-start(bf16[256,1536]{0,1:T(8,128)(2,1)S(1)} %get-tuple-element.518), channel_id=1, source_target_pairs={{0,6},{1,7},{2,8},{3,9},{4,10},{5,11},{6,12},{7,13},{8,14},{9,15},... | collective-permute-start | bytes 2359304 | tf_op jit(solution)/shard_map/ppermute | solution.py:18
  1593.7 179.3 %reduce-scatter.37.cloned.1.call-start = ((), (), s32[]{:S(2)}) async-start(), calls=%async_computation.19 | async-start | bytes 5308416 | tf_op jit(solution)/shard_map/reduce_scatter | solution.py:318
  1600.1 230.1 %reduce-scatter.41.cloned.1.call-start = ((), (), s32[]{:S(2)}) async-start(), calls=%async_computation.21 | async-start | bytes 5308416 | tf_op jit(solution)/shard_map/reduce_scatter | solution.py:324
  1606.1 281.2 %reduce-scatter.39.cloned.1.call-start = ((), (), s32[]{:S(2)}) async-start(), calls=%async_computation.20 | async-start | bytes 5308416 | tf_op jit(solution)/shard_map/reduce_scatter | solution.py:324
  1611.5 332.9 %reduce-scatter.35.cloned.1.call-start = ((), (), s32[]{:S(2)}) async-start(), calls=%async_computation.18 | async-start | bytes 5308416 | tf_op jit(solution)/shard_map/reduce_scatter | solution.py:318
  1617.3 363.7 %reduce-scatter.53.cloned.1.call-start = ((), (), s32[]{:S(2)}) async-start(), calls=%async_computation.35 | async-start | bytes 221184
  1620.3 397.8 %reduce-scatter.49.cloned.1.call-start = ((), (), s32[]{:S(2)}) async-start(), calls=%async_computation.33 | async-start | bytes 221184
  1621.2 434.2 %reduce-scatter.45.cloned.1.call-start = ((), (), s32[]{:S(2)}) async-start(), calls=%async_computation.31 | async-start | bytes 221184
  1622.3 469.7 %reduce-scatter.51.cloned.1.call-start = ((), (), s32[]{:S(2)}) async-start(), calls=%async_computation.34 | async-start | bytes 221184
  1627.8 500.9 %reduce-scatter.47.cloned.1.call-start = ((), (), s32[]{:S(2)}) async-start(), calls=%async_computation.32 | async-start | bytes 221184
  1628.7 537.2 %reduce-scatter.43.cloned.1.call-start = ((), (), s32[]{:S(2)}) async-start(), calls=%async_computation.30 | async-start | bytes 221184
  1629.7 673.2 %all-reduce.11.cloned.1.call-start = ((), (), s32[]{:S(2)}) async-start(), calls=%async_computation.36 | async-start | bytes 7077888 | tf_op jit(solution)/shard_map/psum | solution.py:338
  (167 other events, 7498.1 us)
Sparse Core Ops, SparseCore 0:
  10.5 38.1 all-gather.26
  50.5 24.4 all-gather.28
  77.5 40.9 all-gather.30
  120.8 38.9 all-gather.32
  162.1 33.7 all-gather.34
  197.6 56.4 all-gather.36
  256.6 47.6 all-gather.38
  529.1 74.4 all-gather.40
  1150.8 48.1 reduce-scatter.32
  1208.8 77.4 reduce-scatter.30
  1350.3 98.4 reduce-scatter.28
  1593.9 121.8 reduce-scatter.26
  1719.2 53.7 reduce-scatter.36
  1776.3 53.7 reduce-scatter.40
  1833.5 53.7 reduce-scatter.38
  1890.6 53.7 reduce-scatter.34
  1947.2 33.6 reduce-scatter.52
  1984.4 33.6 reduce-scatter.48
  2021.7 33.6 reduce-scatter.44
  2058.2 33.6 reduce-scatter.50
  2095.0 33.6 reduce-scatter.46
  2132.2 33.6 reduce-scatter.42
  2168.9 133.9 all-reduce.10
where the time goes:
time: 2330 us; the launch traced here: 2320 us
  waiting for transfers between devices  1060 us (45%)
  starting transfers between devices  398 us (17%)
  matrix products  349 us (15%)
  other arithmetic  174 us (7%)
  blocking collectives  168 us (7%)
  local copies, waits for them, and re-layouts  143 us (6%)
    ppermute x60, waiting for transfers between devices, passed_along(): lax.ppermute(value, axis, [(source, source + steps) for source in range(l...  440 us
    ppermute x60, starting transfers between devices, passed_along(): lax.ppermute(value, axis, [(source, source + steps) for source in range(l...  397 us
    unnamed x29, waiting for transfers between devices  188 us
    psum x1, waiting for transfers between devices, local(): lax.psum(summed[0].astype(jnp.bfloat16), 'rep').astype(jnp.float32)  121 us
    reduce_scatter x2, waiting for transfers between devices, local(): lax.psum_scatter(grads[3].astype(jnp.bfloat16), 'group', scatter_dimensio...  114 us
    reduce_scatter x2, waiting for transfers between devices, local(): lax.psum_scatter(grads[5].astype(jnp.bfloat16), 'group', scatter_dimensio...  114 us
    reduce_scatter x2, waiting for transfers between devices, local(): lax.psum_scatter(grads[0].astype(jnp.bfloat16), 'group', scatter_dimensio...  85.8 us
    all_gather x2, blocking collectives, local(): lax.all_gather(fc1_bias[layer_at], 'group', axis=0, tiled=True)  58.5 us
  transfers between devices with their start and end apart: 83, of which 26 were waited for; matrix products, arithmetic and copies ran while one was open for 21% of the time, Pallas kernels for 0%

commit v1 on v0

v1 whole, which is shorter than its diff:
```python
import functools

import jax
import jax.numpy as jnp
from jax import lax
from jax.experimental import pallas as pl
from jax.experimental.pallas import tpu as pltpu
from jax.sharding import PartitionSpec as P

H = 12
HD = 64
LAYERS = 2
MAXLEN = 1500
SPLIT = 4
HEADS = H // SPLIT
WIDE = HEADS * HD
QROWS = 256
KROWS = 512
EPSILON = 1e-05
AXES = ("group", "rep")
NT = (((1,), (1,)), ((), ()))
NN = (((1,), (0,)), ((), ()))
TN = (((0,), (0,)), ((), ()))


def dot32(a, b, dims):
    return lax.dot_general(a, b, dims, preferred_element_type=jnp.float32)


def layer_norm(values, gain, offset):
    center = jnp.mean(values, axis=-1, keepdims=True)
    shifted = values - center
    spread = jnp.mean(shifted * shifted, axis=-1, keepdims=True)
    inverse = lax.rsqrt(spread + EPSILON)
    unit_rows = shifted * inverse
    return (unit_rows * gain + offset, unit_rows, inverse)


def norm_back(upstream, unit_rows, inverse, gain):
    scaled = upstream * gain
    result = inverse * (
        scaled
        - jnp.mean(scaled, axis=-1, keepdims=True)
        - unit_rows * jnp.mean(scaled * unit_rows, axis=-1, keepdims=True)
    )
    return (result, jnp.sum(upstream * unit_rows, axis=0), jnp.sum(upstream, axis=0))


def gelu_slope(inputs):
    normal_cdf = 0.5 * (1.0 + lax.erf(inputs * 0.7071067811865476))
    return normal_cdf + inputs * jnp.exp(-0.5 * inputs * inputs) * 0.3989422804014327


def head_rows(rows):
    lane = lax.broadcasted_iota(jnp.int32, (rows.shape[0], 2 * HD), 1)
    pair = rows[:, : 2 * HD]
    zero = jnp.zeros_like(pair)
    first = jnp.where(lane < HD, pair, zero)
    second = jnp.where(lane >= HD, pair, zero)
    last = jnp.concatenate([rows[:, 2 * HD :], jnp.zeros((rows.shape[0], HD), rows.dtype)], axis=1)
    return first, second, last


def head_rows_up(rows):
    first, second, _ = head_rows(rows)
    last = jnp.concatenate([jnp.zeros((rows.shape[0], HD), rows.dtype), rows[:, 2 * HD :]], axis=1)
    return first, second, last


KEY_TILE = (0, 0, 1)
VALUE_TILE = (2, 2, 1)


def attend_kernel(bounds, q_ref, kv_ref, low_ref, high_ref, o_ref, lse_ref, top, total, acc):
    block = pl.program_id(0)
    rows = q_ref.shape[0]
    queries = head_rows(q_ref[...])
    low = low_ref[...]
    high = high_ref[...]
    top[...] = jnp.full(top.shape, -1e30, jnp.float32)
    total[...] = jnp.zeros(total.shape, jnp.float32)
    acc[...] = jnp.zeros(acc.shape, jnp.float32)

    def step(at, carry):
        start = pl.multiple_of(at * KROWS, KROWS)
        place = lax.broadcasted_iota(jnp.int32, (rows, KROWS), 1) + start
        allowed = (place >= low) & (place < high)
        tiles = [kv_ref[pl.ds(start, KROWS), 2 * HD * t : 2 * HD * (t + 1)] for t in range(3)]
        for head in range(HEADS):
            scores = dot32(queries[head], tiles[KEY_TILE[head]], NT)
            scores = jnp.where(allowed, scores, -1e30)
            before = top[head]
            now = jnp.maximum(before, jnp.max(scores, axis=1, keepdims=True))
            expd = jnp.exp(scores - now[:, :1])
            fade = jnp.exp(before - now)
            top[head] = now
            total[head] = total[head] * fade + jnp.sum(expd, axis=1, keepdims=True)
            acc[head] = acc[head] * fade + dot32(expd.astype(jnp.bfloat16), tiles[VALUE_TILE[head]], NN)
        return carry

    lax.fori_loop(bounds[block, 0], bounds[block, 1], step, 0)
    lane = lax.broadcasted_iota(jnp.int32, (rows, 2 * HD), 1)
    heard = [acc[head] / total[head] for head in range(HEADS)]
    o_ref[:, : 2 * HD] = jnp.where(lane < HD, heard[0], heard[1])
    o_ref[:, 2 * HD :] = pltpu.roll(heard[2], HD, 1)[:, :HD]
    logs = [top[head] + jnp.log(total[head]) for head in range(HEADS)]
    columns = jnp.where(lane == 0, logs[0], jnp.where(lane == 1, logs[1], logs[2]))
    lse_ref[...] = jnp.transpose(columns)[:8, :]


def attend(queries, window, low, high, bounds):
    rows, span = queries.shape[0], window.shape[0]
    blocks = rows // QROWS
    return pl.pallas_call(
        attend_kernel,
        out_shape=(
            jax.ShapeDtypeStruct((rows, WIDE), jnp.float32),
            jax.ShapeDtypeStruct((8, rows), jnp.float32),
        ),
        grid_spec=pltpu.PrefetchScalarGridSpec(
            num_scalar_prefetch=1,
            grid=(blocks,),
            in_specs=[
                pl.BlockSpec((QROWS, WIDE), lambda i, b: (i, 0)),
                pl.BlockSpec((span, 2 * WIDE), lambda i, b: (0, 0)),
                pl.BlockSpec((QROWS, 1), lambda i, b: (i, 0)),
                pl.BlockSpec((QROWS, 1), lambda i, b: (i, 0)),
            ],
            out_specs=(
                pl.BlockSpec((QROWS, WIDE), lambda i, b: (i, 0)),
                pl.BlockSpec((8, QROWS), lambda i, b: (0, i)),
            ),
            scratch_shapes=[
                pltpu.VMEM((HEADS, QROWS, 2 * HD), jnp.float32),
                pltpu.VMEM((HEADS, QROWS, 2 * HD), jnp.float32),
                pltpu.VMEM((HEADS, QROWS, 2 * HD), jnp.float32),
            ],
        ),
        compiler_params=pltpu.CompilerParams(dimension_semantics=("arbitrary",)),
        cost_estimate=pl.CostEstimate(
            flops=4 * rows * 2000 * WIDE, bytes_accessed=span * WIDE * 4, transcendentals=rows * 2000 * 3
        ),
        name="attend",
    )(bounds, queries, window, low[:, None], high[:, None])


def attend_back_kernel(bounds, q_ref, kv_ref, o_ref, do_ref, lse_ref, range_ref, dq_ref, dkv_ref, grown, dq_acc):
    block = pl.program_id(0)
    rows = q_ref.shape[0]

    @pl.when(block == 0)
    def _():
        grown[...] = jnp.zeros(grown.shape, jnp.float32)

    queries = head_rows(q_ref[...])
    upstream = head_rows_up(do_ref[...])
    product = do_ref[...].astype(jnp.float32) * o_ref[...]
    lane = lax.broadcasted_iota(jnp.int32, (rows, 2 * HD), 1)
    parts = [jnp.sum(p, axis=1, keepdims=True) for p in head_rows(product)]
    columns = jnp.where(lane == 0, parts[0], jnp.where(lane == 1, parts[1], parts[2]))
    deltas = jnp.transpose(columns)[:8, :]
    low, high = range_ref[0:1, :], range_ref[1:2, :]
    dq_acc[...] = jnp.zeros(dq_acc.shape, jnp.float32)

    def step(at, carry):
        start = pl.multiple_of(at * KROWS, KROWS)
        here = pl.ds(start, KROWS)
        place = lax.broadcasted_iota(jnp.int32, (KROWS, rows), 0) + start
        allowed = (place >= low) & (place < high)
        tiles = [kv_ref[here, 2 * HD * t : 2 * HD * (t + 1)] for t in range(3)]
        for head in range(HEADS):
            kt, vt = KEY_TILE[head], VALUE_TILE[head]
            scores = dot32(tiles[kt], queries[head], NT)
            probs = jnp.where(allowed, jnp.exp(scores - lse_ref[head : head + 1, :]), 0.0)
            d_probs = dot32(tiles[vt], upstream[head], NT)
            d_scores = (probs * (d_probs - deltas[head : head + 1, :])).astype(jnp.bfloat16)
            grown[here, 2 * HD * vt : 2 * HD * (vt + 1)] += dot32(probs.astype(jnp.bfloat16), upstream[head], NN)
            grown[here, 2 * HD * kt : 2 * HD * (kt + 1)] += dot32(d_scores, queries[head], NN)
            dq_acc[head] += dot32(d_scores, tiles[kt], TN)
        return carry

    lax.fori_loop(bounds[block, 0], bounds[block, 1], step, 0)
    dq_ref[:, : 2 * HD] = jnp.where(lane < HD, dq_acc[0], dq_acc[1])
    dq_ref[:, 2 * HD :] = dq_acc[2][:, :HD]

    @pl.when(block == pl.num_programs(0) - 1)
    def _():
        dkv_ref[...] = grown[...].astype(jnp.bfloat16)


def attend_back(queries, window, heard, d_heard, lse, ranges, bounds):
    rows, span = queries.shape[0], window.shape[0]
    blocks = rows // QROWS
    return pl.pallas_call(
        attend_back_kernel,
        out_shape=(
            jax.ShapeDtypeStruct((rows, WIDE), jnp.float32),
            jax.ShapeDtypeStruct((span, 2 * WIDE), jnp.bfloat16),
        ),
        grid_spec=pltpu.PrefetchScalarGridSpec(
            num_scalar_prefetch=1,
            grid=(blocks,),
            in_specs=[
                pl.BlockSpec((QROWS, WIDE), lambda i, b: (i, 0)),
                pl.BlockSpec((span, 2 * WIDE), lambda i, b: (0, 0)),
                pl.BlockSpec((QROWS, WIDE), lambda i, b: (i, 0)),
                pl.BlockSpec((QROWS, WIDE), lambda i, b: (i, 0)),
                pl.BlockSpec((8, QROWS), lambda i, b: (0, i)),
                pl.BlockSpec((8, QROWS), lambda i, b: (0, i)),
            ],
            out_specs=(
                pl.BlockSpec((QROWS, WIDE), lambda i, b: (i, 0)),
                pl.BlockSpec((span, 2 * WIDE), lambda i, b: (0, 0)),
            ),
            scratch_shapes=[
                pltpu.VMEM((span, 2 * WIDE), jnp.float32),
                pltpu.VMEM((HEADS, QROWS, 2 * HD), jnp.float32),
            ],
        ),
        compiler_params=pltpu.CompilerParams(dimension_semantics=("arbitrary",)),
        cost_estimate=pl.CostEstimate(
            flops=10 * rows * 2000 * WIDE, bytes_accessed=span * WIDE * 12, transcendentals=rows * 2000 * 3
        ),
        name="attend_back",
    )(bounds, queries, window, heard, d_heard, lse, ranges)


class Plan:
    def __init__(self, groups, reps):
        self.groups, self.reps = groups, reps
        self.count = groups * reps
        self.outer = groups // (2 * SPLIT)
        self.sequences = self.count // SPLIT

    def split(self, flat):
        return flat // self.reps // 2 % SPLIT

    def sequence(self, flat):
        group, rep = flat // self.reps, flat % self.reps
        return (group // (2 * SPLIT) * self.reps + rep) * 2 + group % 2

    def device(self, sequence, split):
        core, rest = sequence % 2, sequence // 2
        rep, outer = rest % self.reps, rest // self.reps
        return ((outer * SPLIT + split) * 2 + core) * self.reps + rep

    def inward(self, value):
        return lax.ppermute(value, AXES, [(f, self.device(f // SPLIT, f % SPLIT)) for f in range(self.count)])

    def outward(self, value):
        return lax.ppermute(value, AXES, [(self.device(f // SPLIT, f % SPLIT), f) for f in range(self.count)])

    def across(self, value, mask):
        pairs = [(f, self.device(self.sequence(f), self.split(f) ^ mask)) for f in range(self.count)]
        return lax.ppermute(value, AXES, pairs)

    def along(self, value, steps):
        pairs = [
            (f, self.device(self.sequence(f) + steps, self.split(f)))
            for f in range(self.count)
            if 0 <= self.sequence(f) + steps < self.sequences
        ]
        return lax.ppermute(value, AXES, pairs)

    def beside(self, value, mask):
        pairs = []
        for f in range(self.count):
            group, rep = f // self.reps, f % self.reps
            outer, split, core = group // (2 * SPLIT), group // 2 % SPLIT, group % 2
            mate = (outer * 2 + core) ^ mask
            pairs.append((f, ((mate // 2 * SPLIT + split) * 2 + mate % 2) * self.reps + rep))
        return lax.ppermute(value, AXES, pairs)

    def least(self, value):
        bit = 1
        while bit < self.count:
            value = jnp.minimum(value, lax.ppermute(value, AXES, [(f, f ^ bit) for f in range(self.count)]))
            bit *= 2
        return value


def collect(plan, piece, split):
    rows = piece.shape[0]
    whole = jnp.zeros((SPLIT * rows,) + piece.shape[1:], piece.dtype)
    parts = [piece] + [plan.across(piece, mask) for mask in range(1, SPLIT)]
    for mask, part in enumerate(parts):
        whole = lax.dynamic_update_slice_in_dim(whole, part, (split ^ mask) * rows, 0)
    return whole


def deal(plan, whole, split):
    rows = whole.shape[0] // SPLIT
    own = lax.dynamic_slice_in_dim(whole, split * rows, rows, 0)
    return [own] + [
        plan.across(lax.dynamic_slice_in_dim(whole, (split ^ mask) * rows, rows, 0), mask) for mask in range(1, SPLIT)
    ]


def by_split(parts, split, axis):
    stacked = jnp.stack(parts)
    return jnp.concatenate(
        [lax.dynamic_index_in_dim(stacked, split ^ k, 0, keepdims=False) for k in range(SPLIT)], axis=axis
    )


def value_order(columns):
    return jnp.concatenate([columns[..., 2 * HD :], columns[..., : 2 * HD]], axis=-1)


def value_back(columns):
    return jnp.concatenate([columns[..., HD:], columns[..., :HD]], axis=-1)


def local(plan, *arguments):
    (tokens, segments, w_in, b_attn, w_out, w_up, b_up, w_down, b_down, gains, offsets, cotangent) = arguments
    rows, width = tokens.shape
    hidden = b_up.shape[1] * plan.groups
    reach = -(-(MAXLEN - 1 - SPLIT * rows) // KROWS) * KROWS
    block_rows = SPLIT * rows
    score_scale = HD ** (-0.5)
    flat = lax.axis_index("group") * plan.reps + lax.axis_index("rep")
    group = lax.axis_index("group")
    split = plan.split(flat)
    sequence = plan.sequence(flat)
    mate = group // (2 * SPLIT) * 2 + group % 2
    everything = rows * plan.count

    clips = everything // MAXLEN
    place = lax.iota(jnp.int32, rows) + flat * rows
    hits = segments[None, :] == lax.iota(jnp.int32, clips)[:, None]
    starts = jnp.min(jnp.where(hits, place[None, :], everything), axis=1)
    starts = jnp.pad(starts, (0, 128 - clips), constant_values=everything)[None, :]
    resid = plan.inward(tokens)
    starts = plan.least(starts)[0, :clips]
    own_place = lax.iota(jnp.int32, block_rows) + sequence * block_rows
    begun = jnp.where(starts[None, :] <= own_place[:, None], starts[None, :], -everything)
    begun = jnp.max(begun, axis=1)
    inside = own_place < begun + MAXLEN
    origin = sequence * block_rows - block_rows - reach
    low = jnp.where(inside, begun, own_place) - origin
    high = jnp.where(inside, begun + MAXLEN, own_place + 1) - origin
    first_block = jnp.min(low.reshape(-1, QROWS), axis=1) // KROWS
    last_block = (jnp.max(high.reshape(-1, QROWS), axis=1) + KROWS - 1) // KROWS
    bounds = jnp.stack([first_block, last_block], axis=1)
    ranges = jnp.pad(jnp.stack([low, high]), ((0, 6), (0, 0)))

    shard = w_in.shape[1]
    columns = w_in.reshape(LAYERS, shard, 3, SPLIT, WIDE)
    columns = jnp.stack([columns[:, :, 0], columns[:, :, 1], value_order(columns[:, :, 2])], axis=2)
    columns = columns.transpose(3, 0, 1, 2, 4).reshape(SPLIT, LAYERS * shard, 3 * WIDE)
    vectors = jnp.concatenate(
        [
            b_attn.reshape(LAYERS, -1),
            gains.reshape(LAYERS, -1),
            offsets.reshape(LAYERS, -1),
            b_up.reshape(LAYERS, -1),
            b_down.reshape(LAYERS, -1),
        ],
        axis=1,
    )
    each = vectors.shape[1]
    rows_of = -(-LAYERS * each // (3 * WIDE))
    flat_vectors = jnp.pad(vectors.reshape(-1), (0, rows_of * 3 * WIDE - LAYERS * each)).reshape(rows_of, 3 * WIDE)
    payload = jnp.concatenate([columns, jnp.broadcast_to(flat_vectors, (SPLIT,) + flat_vectors.shape)], axis=1)
    depth = payload.shape[1]
    arrived = jnp.stack(deal(plan, payload.reshape(SPLIT * depth, 3 * WIDE), split))
    mates = plan.groups // SPLIT
    arrived = jnp.stack([arrived] + [plan.beside(arrived, mask) for mask in range(1, mates)])
    pieces = []
    for member in range(plan.groups):
        member_split = member // 2 % SPLIT
        member_mate = member // (2 * SPLIT) * 2 + member % 2
        pieces.append(arrived[member_mate ^ mate, member_split ^ split])
    in_weights = jnp.concatenate(
        [piece[: LAYERS * shard].reshape(LAYERS, shard, 3 * WIDE) for piece in pieces], axis=1
    )
    vectors = jnp.stack(
        [piece[LAYERS * shard :].reshape(-1)[: LAYERS * each].reshape(LAYERS, each) for piece in pieces], axis=1
    ).astype(jnp.float32)

    def whole_vector(layer, start, size):
        return vectors[layer, :, start : start + size].reshape(-1)

    piece = width // plan.groups

    resid = resid.astype(jnp.float32)
    stored = []
    for layer in range(LAYERS):
        full_out = lax.all_gather(w_out[layer], "group", axis=0, tiled=True)
        full_up = lax.all_gather(w_up[layer], "group", axis=0, tiled=True)
        full_down = lax.all_gather(w_down[layer], "group", axis=0, tiled=True)
        bias = [whole_vector(layer, k * piece, piece) for k in range(3)]
        gain = [whole_vector(layer, (3 + k) * piece, piece) for k in range(2)]
        offset = [whole_vector(layer, (5 + k) * piece, piece) for k in range(2)]
        up_bias = whole_vector(layer, 7 * piece, hidden // plan.groups)
        down_bias = whole_vector(layer, 7 * piece + hidden // plan.groups, piece)
        query_bias = lax.dynamic_slice_in_dim(bias[0], split * WIDE, WIDE)
        value_bias = value_order(lax.dynamic_slice_in_dim(bias[1], split * WIDE, WIDE))

        normed, unit_first, inverse_first = layer_norm(resid, gain[0], offset[0])
        first = collect(plan, normed.astype(jnp.bfloat16), split)
        mixed = dot32(first, in_weights[layer], NN)
        queries = ((mixed[:, :WIDE] + query_bias) * score_scale).astype(jnp.bfloat16)
        add = jnp.concatenate([jnp.zeros((WIDE,), jnp.float32), value_bias])
        key_value = (mixed[:, WIDE:] + add).astype(jnp.bfloat16)
        window = jnp.concatenate(
            [
                plan.along(key_value[-reach:], 2),
                plan.along(key_value, 1),
                key_value,
                plan.along(key_value, -1),
                plan.along(key_value[:reach], -2),
            ],
            axis=0,
        )
        attended, lse = attend(queries, window, low, high, bounds)
        heard = by_split(deal(plan, attended.astype(jnp.bfloat16), split), split, 1)
        middle = resid + dot32(heard, full_out, NN) + bias[2]
        normed, unit_second, inverse_second = layer_norm(middle, gain[1], offset[1])
        second = normed.astype(jnp.bfloat16)
        pre_act = dot32(second, full_up, NN) + up_bias
        active = jax.nn.gelu(pre_act, approximate=False).astype(jnp.bfloat16)
        resid = middle + dot32(active, full_down, NN) + down_bias
        stored.append(
            (unit_first, inverse_first, first, queries, window, attended, lse, heard, unit_second, inverse_second)
            + (second, pre_act, active, full_out, full_up, full_down, gain)
        )
    output = plan.outward(resid.astype(jnp.bfloat16)).astype(jnp.float32)

    upstream = plan.inward(cotangent).astype(jnp.float32)
    shares = [None] * LAYERS
    small = [None] * LAYERS
    for layer in reversed(range(LAYERS)):
        (unit_first, inverse_first, first, queries, window, attended, lse, heard, unit_second, inverse_second) = stored[
            layer
        ][:10]
        second, pre_act, active, full_out, full_up, full_down, gain = stored[layer][10:]
        down_rounded = upstream.astype(jnp.bfloat16)
        g_down_b = jnp.sum(upstream, axis=0)
        g_down = dot32(active, down_rounded, TN).astype(jnp.bfloat16)
        d_pre = dot32(down_rounded, full_down, NT) * gelu_slope(pre_act)
        up_rounded = d_pre.astype(jnp.bfloat16)
        g_up_b = jnp.sum(d_pre, axis=0)
        g_up = dot32(second, up_rounded, TN).astype(jnp.bfloat16)
        d_second = dot32(up_rounded, full_up, NT)
        d_norm, g_gain_two, g_offset_two = norm_back(d_second, unit_second, inverse_second, gain[1])
        d_middle = upstream + d_norm
        middle_rounded = d_middle.astype(jnp.bfloat16)
        g_out_b = jnp.sum(d_middle, axis=0)
        g_out = dot32(heard, middle_rounded, TN).astype(jnp.bfloat16)
        d_heard = dot32(middle_rounded, full_out, NT).astype(jnp.bfloat16)
        by_head = d_heard.reshape(rows, SPLIT, WIDE).transpose(1, 0, 2).reshape(SPLIT * rows, WIDE)
        d_attended = by_split(deal(plan, by_head, split), split, 0)
        d_query, d_window = attend_back(queries, window, attended, d_attended, lse, ranges, bounds)
        d_own = d_window[reach + block_rows : reach + 2 * block_rows].astype(jnp.float32)
        d_own = d_own + plan.along(d_window[reach : reach + block_rows], -1).astype(jnp.float32)
        d_own = d_own + plan.along(d_window[reach + 2 * block_rows : reach + 3 * block_rows], 1).astype(jnp.float32)
        from_next = plan.along(d_window[:reach], -2).astype(jnp.float32)
        from_last = plan.along(d_window[reach + 3 * block_rows :], 2).astype(jnp.float32)
        d_own = d_own.at[block_rows - reach :].add(from_next).at[:reach].add(from_last)
        d_query = d_query * score_scale
        d_mixed = jnp.concatenate([d_query, d_own], axis=1)
        mixed_rounded = d_mixed.astype(jnp.bfloat16)
        sums = jnp.sum(d_mixed, axis=0)
        g_in = dot32(first, mixed_rounded, TN).astype(jnp.bfloat16)
        d_first_part = dot32(mixed_rounded, in_weights[layer], NT).astype(jnp.bfloat16)
        d_first = sum(part.astype(jnp.float32) for part in deal(plan, d_first_part, split))
        d_norm, g_gain_one, g_offset_one = norm_back(d_first, unit_first, inverse_first, gain[0])
        upstream = d_middle + d_norm

        came = lax.all_to_all(g_in.reshape(plan.groups, shard, 3 * WIDE), "group", 0, 0, tiled=True)
        came = came.reshape(plan.outer, SPLIT, 2, shard, 3, WIDE).astype(jnp.float32)
        came = jnp.sum(came, axis=(0, 2))
        came = jnp.stack([came[:, :, 0], came[:, :, 1], value_back(came[:, :, 2])], axis=2)
        g_in = came.transpose(1, 2, 0, 3).reshape(shard, 3 * width).astype(jnp.bfloat16)
        g_out = lax.psum_scatter(g_out, "group", scatter_dimension=0, tiled=True)
        g_up = lax.psum_scatter(g_up, "group", scatter_dimension=0, tiled=True)
        g_down = lax.psum_scatter(g_down, "group", scatter_dimension=0, tiled=True)
        shares[layer] = (g_in, g_out, g_up, g_down)
        blank = jnp.zeros((width,), jnp.float32)
        g_query_b = lax.dynamic_update_slice_in_dim(blank, sums[:WIDE], split * WIDE, 0)
        g_value_b = lax.dynamic_update_slice_in_dim(blank, value_back(sums[2 * WIDE :]), split * WIDE, 0)
        small[layer] = jnp.concatenate(
            [
                v.reshape(plan.groups, -1)
                for v in (
                    g_query_b,
                    g_value_b,
                    g_out_b,
                    g_gain_one,
                    g_gain_two,
                    g_offset_one,
                    g_offset_two,
                    g_up_b,
                    g_down_b,
                )
            ],
            axis=1,
        )
    input_grad = plan.outward(upstream.astype(jnp.bfloat16)).astype(jnp.float32)
    grads = []
    for field in range(4):
        grads.append(
            jnp.stack([lax.psum(shares[layer][field], "rep").astype(jnp.float32) for layer in range(LAYERS)])
        )
    small = lax.psum(jnp.stack(small, axis=1), AXES)
    small = lax.dynamic_index_in_dim(small, group, 0, keepdims=False)
    g_bias = small[:, : 3 * piece].reshape(LAYERS, 3, piece)
    g_gain = small[:, 3 * piece : 5 * piece].reshape(LAYERS, 2, piece)
    g_offset = small[:, 5 * piece : 7 * piece].reshape(LAYERS, 2, piece)
    g_up_b = small[:, 7 * piece : 7 * piece + hidden // plan.groups]
    g_down_b = small[:, 7 * piece + hidden // plan.groups :]
    return (
        output,
        input_grad,
        grads[0],
        g_bias,
        grads[1],
        grads[2],
        g_up_b,
        grads[3],
        g_down_b,
        g_gain,
        g_offset,
    )


def solution(mesh):
    both = P(AXES, None)
    in_specs = (
        both,
        P(AXES),
        P(None, "group", None),
        P(None, None, "group"),
        P(None, "group", None),
        P(None, "group", None),
        P(None, "group"),
        P(None, "group", None),
        P(None, "group"),
        P(None, None, "group"),
        P(None, None, "group"),
        both,
    )
    out_specs = (
        both,
        both,
        P(None, "group", None),
        P(None, None, "group"),
        P(None, "group", None),
        P(None, "group", None),
        P(None, "group"),
        P(None, "group", None),
        P(None, "group"),
        P(None, None, "group"),
        P(None, None, "group"),
    )
    plan = Plan(mesh.shape["group"], mesh.shape["rep"])
    return jax.shard_map(
        functools.partial(local, plan), mesh=mesh, in_specs=in_specs, out_specs=out_specs, check_vma=False
    )
```

time: 2330 us -> 1070 us (0.46)
  waiting for transfers between devices: 1060 us -> 603 us
  starting transfers between devices: 398 us -> 100 us
  matrix products: 349 us -> 93.1 us
  blocking collectives: 168 us -> 0 us
  other arithmetic: 174 us -> 53.5 us
  Pallas kernels: 0 us -> 96.4 us
  local copies, waits for them, and re-layouts: 143 us -> 93.5 us
    ppermute x60 -> x53, starting transfers between devices: 397 us -> 91 us  [the longest x16 48.7 us: along(): return lax.ppermute(value, AXES, pairs)]
    ppermute x60 -> x53, waiting for transfers between devices: 440 us -> 184 us  [the longest x27 81.6 us: across(): return lax.ppermute(value, AXES, pairs)]
    dot_general x108 -> x24, matrix products: 349 us -> 93.1 us  [dot32(): return lax.dot_general(a, b, dims, preferred_element_type=jnp.float32)]
    unnamed x29 -> x14, waiting for transfers between devices: 188 us -> 1.25 us
    reduce_scatter x8 -> x6, waiting for transfers between devices: 314 us -> 129 us  [the longest x2 71.5 us: local(): g_down = lax.psum_scatter(g_down, 'group', scatter_dimension=0, tiled=True)]
    psum x1 -> x2, waiting for transfers between devices: 121 us -> 274 us  [the longest x1 140 us: local(): small = lax.psum(jnp.stack(small, axis=1), AXES)]
    all_gather x8 -> x0, blocking collectives: 119 us -> none  [the longest x2 58.5 us: local(): lax.all_gather(fc1_bias[layer_at], 'group', axis=0, tiled=True)]
    pallas_call x0 -> x4, Pallas kernels: none -> 96.4 us  [the longest x2 48.6 us: attend(): pl.pallas_call(attend_kernel, out_shape=(jax.ShapeDtypeStruct((rows, WIDE...]
  transfers between devices with their start and end apart: 83 -> 69, of which waited for: 26 -> 35; matrix products, arithmetic and copies ran while one was open for 21% -> 20% of each run, Pallas kernels for 0% -> 7%
where the time goes in v1:
time: 1070 us; the launch traced here: 1060 us
  waiting for transfers between devices  603 us (56%)
  starting transfers between devices  100 us (9%)
  Pallas kernels  96.4 us (9%)
  local copies, waits for them, and re-layouts  93.5 us (9%)
  matrix products  93.1 us (9%)
  other arithmetic  53.5 us (5%)
  between operations  16.5 us (2%)
    psum x1, waiting for transfers between devices, local(): small = lax.psum(jnp.stack(small, axis=1), AXES)  140 us
    psum x1, waiting for transfers between devices, local(): lax.psum(shares[layer][field], 'rep').astype(jnp.float32)  134 us
    dot_general x24, matrix products, dot32(): return lax.dot_general(a, b, dims, preferred_element_type=jnp.float32)  93.1 us
    ppermute x27, waiting for transfers between devices, across(): return lax.ppermute(value, AXES, pairs)  81.6 us
    reduce_scatter x2, waiting for transfers between devices, local(): g_down = lax.psum_scatter(g_down, 'group', scatter_dimension=0, tiled=True)  71.5 us
    ppermute x16, waiting for transfers between devices, along(): return lax.ppermute(value, AXES, pairs)  63.8 us
    reduce_scatter x2, waiting for transfers between devices, local(): g_up = lax.psum_scatter(g_up, 'group', scatter_dimension=0, tiled=True)  57.1 us
    ppermute x16, starting transfers between devices, along(): return lax.ppermute(value, AXES, pairs)  48.7 us
  transfers between devices with their start and end apart: 69, of which 35 were waited for; matrix products, arithmetic and copies ran while one was open for 20% of the time, Pallas kernels for 7%

profile of v1, /device:TPU:0, one launch (start us, length us, event | category | flops | bytes accessed | tf_op | source)
XLA Modules:
  0.0 1056.2 jit_solution(908903998353616725)
XLA Ops:
  9.1 2.4 fusion.166
  25.6 4.0 collective-permute-start.8
  31.1 4.6 collective-permute-start.1
  36.1 24.3 %collective-permute-done.1 = s32[1,128]{1,0:T(1,128)S(1)} collective-permute-done((s32[1,128]{1,0:T(1,128)S(1)}, s32[1,128]{1,0:T(1,128)S(1)}, u32[]{:S(2)}, u32[]{:S(2)}) %collective-permute-start.1) | collective-permute-done | bytes 544 | tf_op jit(solution)/shard_map/ppermute | solution.py:277
  60.4 4.4 collective-permute-done.2
  66.0 3.6 collective-permute-done.4
  69.6 3.7 collective-permute-done.5
  83.7 2.6 collective-permute-start.12
  89.6 13.7 %collective-permute-done.10 = bf16[256,768]{1,0:T(8,128)(2,1)} collective-permute-done((bf16[256,768]{1,0:T(8,128)(2,1)S(1)}, bf16[256,768]{1,0:T(8,128)(2,1)}, u32[]{:S(2)}, u32[]{:S(2)}) %collective-permute-start.10) | collective-permute-done | bytes 393248 | tf_op jit(solution)/shard_map/ppermute | solution.py:255
  106.8 6.2 collective-permute-done.12
  113.8 3.1 fusion.93
  118.2 2.6 collective-permute-start.14
  123.0 2.7 collective-permute-start.13
  130.2 5.3 collective-permute-done.13
  137.5 12.4 %collective-permute-done.16 = bf16[512,384]{1,0:T(8,128)(2,1)S(1)} collective-permute-done((bf16[512,384]{1,0:T(8,128)(2,1)}, bf16[512,384]{1,0:T(8,128)(2,1)S(1)}, u32[]{:S(2)}, u32[]{:S(2)}) %collective-permute-start.16) | collective-permute-done | bytes 393248 | tf_op jit(solution)/shard_map/ppermute | solution.py:263
  151.8 24.2 %attend.2 = (f32[1024,192]{1,0:T(8,128)}, f32[8,1024]{1,0:T(8,128)}) custom-call(s32[4,2]{1,0:T(4,128)} %pad_add_fusion.1.bounds, bf16[1024,192]{1,0:T(8,128)(2,1)} %fusion.86.q_ref, bf16[4096,384]{1,0:T(8,128)(2,1)} %copy-done.50, s32[1024,1]{1,0:T(8,128)} %get-tuple-element.237.low_ref, s32[1024,1]{1,0:T(8,128)} %get-tuple-element.236.high_ref), custom_call_target="tpu_custom_call" | custom-call | flops 1572864000 | bytes 3145728 | tf_op jit(solution)/shard_map/attend/pallas_call | solution.py:114
  178.5 2.4 collective-permute-start.19
  187.0 11.0 %fusion.30 = (bf16[256,3072]{1,0:T(8,128)(2,1)S(1)}, f32[256,3072]{1,0:T(8,128)}) fusion(f32[3072]{0:T(1024)S(1)} %bitcast.268, bf16[1,768,3072]{2,1,0:T(8,128)(2,1)} %all-gather.15.cloned.1.call-done, f32[256,768]{1,0:T(8,128)S(1)} %get-tuple-element.266, f32[768]{0:T(1024)S(1)} %add.633, f32[768]{0:T(1024)S(1)} %mul.366, f32[256]{0:T(256)S(1)} %add_rsqrt_fusion.2, ...), kind=kOutput, calls=%fused_computation.46 | convolution fusion | flops 1260847104 | bytes 10244096 | tf_op jit(solution)/shard_map/dot_general | solution.py:27
  198.1 4.3 fusion.173
  206.6 14.9 %collective-permute-done.20 = bf16[256,768]{1,0:T(8,128)(2,1)S(1)} collective-permute-done((bf16[256,768]{1,0:T(8,128)(2,1)S(1)}, bf16[256,768]{1,0:T(8,128)(2,1)S(1)}, u32[]{:S(2)}, u32[]{:S(2)}) %collective-permute-start.20) | collective-permute-done | bytes 393248 | tf_op jit(solution)/shard_map/ppermute | solution.py:255
  222.4 7.8 collective-permute-done.22
  236.2 4.4 collective-permute-start.23
  254.4 33.9 %collective-permute-done.26 = bf16[512,384]{1,0:T(8,128)(2,1)S(1)} collective-permute-done((bf16[512,384]{1,0:T(8,128)(2,1)}, bf16[512,384]{1,0:T(8,128)(2,1)S(1)}, u32[]{:S(2)}, u32[]{:S(2)}) %collective-permute-start.26) | collective-permute-done | bytes 393248 | tf_op jit(solution)/shard_map/ppermute | solution.py:263
  289.1 24.4 %attend.3 = (f32[1024,192]{1,0:T(8,128)}, f32[8,1024]{1,0:T(8,128)}) custom-call(s32[4,2]{1,0:T(4,128)} %pad_add_fusion.1.bounds, bf16[1024,192]{1,0:T(8,128)(2,1)} %fusion.84.q_ref, bf16[4096,384]{1,0:T(8,128)(2,1)} %constant_dynamic-update-slice_fusion.21.kv_ref, s32[1024,1]{1,0:T(8,128)} %get-tuple-element.237.low_ref, s32[1024,1]{1,0:T(8,128)} %get-tuple-element.236.high_ref), custom_call_target="tpu_custom_call" | custom-call | flops 1572864000 | bytes 3145728 | tf_op jit(solution)/shard_map/attend/pallas_call | solution.py:114
  314.9 3.4 collective-permute-start.29
  323.9 11.0 %fusion.33 = (bf16[256,3072]{1,0:T(8,128)(2,1)}, f32[256,3072]{1,0:T(8,128)}) fusion(f32[3072]{0:T(1024)S(1)} %bitcast.267, bf16[1,768,3072]{2,1,0:T(8,128)(2,1)} %all-gather.21.cloned.1.call-done, f32[256,768]{1,0:T(8,128)S(1)} %get-tuple-element.272, f32[768]{0:T(1024)S(1)} %add.656, f32[768]{0:T(1024)S(1)} %mul.382, f32[256]{0:T(256)S(1)} %add_rsqrt_fusion, ...), kind=kOutput, calls=%fused_computation.49 | convolution fusion | flops 1260847104 | bytes 10244096 | tf_op jit(solution)/shard_map/dot_general | solution.py:27
  335.0 7.1 fusion.175
  352.9 2.4 collective-permute-done.34
  356.8 23.7 %attend_back.2 = (f32[1024,192]{1,0:T(8,128)}, bf16[4096,384]{1,0:T(8,128)(2,1)}) custom-call(s32[4,2]{1,0:T(4,128)} %pad_add_fusion.1.bounds, bf16[1024,192]{1,0:T(8,128)(2,1)} %fusion.84.q_ref, bf16[4096,384]{1,0:T(8,128)(2,1)} %constant_dynamic-update-slice_fusion.21.kv_ref, f32[1024,192]{1,0:T(8,128)} %get-tuple-element.68.o_ref, ...), custom_call_target="tpu_custom_call" | custom-call | flops 3932160000 | bytes 9437184 | tf_op jit(solution)/shard_map/attend_back/pallas_call | solution.py:194
  383.6 3.1 collective-permute-start.36
  388.1 14.3 %collective-permute-start.38 = (bf16[512,384]{1,0:T(8,128)(2,1)S(1)}, bf16[512,384]{1,0:T(8,128)(2,1)S(1)}, u32[]{:S(2)}, u32[]{:S(2)}) collective-permute-start(bf16[512,384]{1,0:T(8,128)(2,1)S(1)} %get-tuple-element.188), channel_id=1, source_target_pairs={{0,1},{1,2},{2,3},{4,5},{5,6},{6,7},{8,9},{9,10},{10,11},{12,13},{... | collective-permute-start | bytes 1179656 | tf_op jit(solution)/shard_map/ppermute | solution.py:263
  402.8 11.6 %collective-permute-done.37 = bf16[512,384]{1,0:T(8,128)(2,1)S(1)} collective-permute-done((bf16[512,384]{1,0:T(8,128)(2,1)S(1)}, bf16[512,384]{1,0:T(8,128)(2,1)S(1)}, u32[]{:S(2)}, u32[]{:S(2)}) %collective-permute-start.37) | collective-permute-done | bytes 393248 | tf_op jit(solution)/shard_map/ppermute | solution.py:263
  423.7 7.0 collective-permute-done.39
  430.7 9.6 collective-permute-done.40
  440.3 2.5 multiply_reduce_fusion.1
  443.8 5.5 fusion.176
  454.6 5.2 convolution_convert_fusion.2
  459.9 5.2 convolution_convert_fusion
  465.1 5.2 convolution_convert_fusion.1
  471.0 5.4 convolution_convert_fusion.3
  483.4 4.3 convolution_convert_fusion.8
  487.7 2.3 copy.224
  490.1 4.4 all-to-all-start.1
  512.4 2.5 collective-permute-done.44
  516.3 24.2 %attend_back.3 = (f32[1024,192]{1,0:T(8,128)}, bf16[4096,384]{1,0:T(8,128)(2,1)}) custom-call(s32[4,2]{1,0:T(4,128)} %pad_add_fusion.1.bounds, bf16[1024,192]{1,0:T(8,128)(2,1)} %fusion.86.q_ref, bf16[4096,384]{1,0:T(8,128)(2,1)} %copy-done.50, f32[1024,192]{1,0:T(8,128)} %get-tuple-element.67.o_ref, bf16[1024,192]{1,0:T(8,128)(2,1)} %pad_maximum_fusion.7.do_ref, ...), custom_call_target="tpu_custom_call" | custom-call | flops 3932160000 | bytes 9437184 | tf_op jit(solution)/shard_map/attend_back/pallas_call | solution.py:194
  540.5 2.8 fusion.162
  544.6 3.9 collective-permute-start.46
  551.9 5.4 collective-permute-start.48
  564.9 2.4 stack.225
  574.9 2.9 collective-permute-start.51
  577.8 4.2 convolution_convert_fusion.9
  585.0 3.6 all-to-all-start
  589.0 3.4 collective-permute-done.50
  592.3 6.2 collective-permute-done.51
  598.5 3.2 fusion.102
  602.9 15.3 %all-to-all-done = bf16[8,96,576]{2,1,0:T(8,128)(2,1)S(1)} async-done(((bf16[8,96,576]{2,1,0:T(8,128)(2,1)}), bf16[8,96,576]{2,1,0:T(8,128)(2,1)S(1)}, u32[]{:S(2)}, u32[]{:S(2)}) %all-to-all-start) | async-done | bytes 884768 | tf_op jit(solution)/shard_map/all_to_all | solution.py:471
  622.0 2.4 stack.222
  624.3 14.3 %reduce-scatter.17.cloned.1.call-done = bf16[384,768]{1,0:T(8,128)(2,1)} async-done(((bf16[3072,768]{1,0:T(8,128)(2,1)}), bf16[384,768]{1,0:T(8,128)(2,1)}) %reduce-scatter.17.cloned.1.call-update) | async-done | bytes 589840 | tf_op jit(solution)/shard_map/reduce_scatter | solution.py:478
  638.6 57.3 %reduce-scatter.15.cloned.1.call-done = bf16[384,768]{1,0:T(8,128)(2,1)} async-done(((bf16[3072,768]{1,0:T(8,128)(2,1)}), bf16[384,768]{1,0:T(8,128)(2,1)}) %reduce-scatter.15.cloned.1.call-update) | async-done | bytes 589840 | tf_op jit(solution)/shard_map/reduce_scatter | solution.py:478
  695.9 57.1 %reduce-scatter.11.cloned.1.call-done = bf16[96,3072]{1,0:T(8,128)(2,1)} async-done(((bf16[768,3072]{1,0:T(8,128)(2,1)}), bf16[96,3072]{1,0:T(8,128)(2,1)}) %reduce-scatter.11.cloned.1.call-update) | async-done | bytes 589840 | tf_op jit(solution)/shard_map/reduce_scatter | solution.py:477
  753.7 4.5 fusion.76
  763.6 139.7 %all-reduce.6.cloned.1.call-done = f32[8,2,1152]{2,1,0:T(2,128)} async-done(((f32[8,2,1152]{2,1,0:T(2,128)}), f32[8,2,1152]{2,1,0:T(2,128)}) %all-reduce.6.cloned.1.call-update) | async-done | bytes 73744 | tf_op jit(solution)/shard_map/psum | solution.py:506
  908.2 134.5 %all-reduce.8.cloned.1.call-done = (bf16[1,96,2304]{2,1,0:T(8,128)(2,1)}, bf16[1,96,2304]{2,1,0:T(8,128)(2,1)}, bf16[1,96,768]{2,1,0:T(8,128)(2,1)}, bf16[1,96,7...) async-done(((bf16[1,96,2304]{2,1,0:T(8,128)(2,1)}, ...) | async-done | bytes 3538960 | tf_op jit(solution)/shard_map/psum | solution.py:504
  1042.7 3.0 maximum_convert_fusion.1
  (614 shorter events, 191.4 us)
Async XLA Ops:
  7.2 177.4 %all-gather.13.cloned.1.call-start = ((), (), s32[]{:S(2)}) async-start(), calls=%async_computation.15 | async-start | bytes 1327104 | tf_op jit(solution)/shard_map/all_gather | solution.py:389
  9.1 177.9 %all-gather.15.cloned.1.call-start = ((), (), s32[]{:S(2)}) async-start(), calls=%async_computation.16 | async-start | bytes 5308416 | tf_op jit(solution)/shard_map/all_gather | solution.py:390
  11.5 186.5 %all-gather.17.cloned.1.call-start = ((), (), s32[]{:S(2)}) async-start(), calls=%async_computation.17 | async-start | bytes 5308416 | tf_op jit(solution)/shard_map/all_gather | solution.py:391
  12.7 308.8 %all-gather.19.cloned.1.call-start = ((), (), s32[]{:S(2)}) async-start(), calls=%async_computation.18 | async-start | bytes 1327104 | tf_op jit(solution)/shard_map/all_gather | solution.py:389
  13.3 310.5 %all-gather.21.cloned.1.call-start = ((), (), s32[]{:S(2)}) async-start(), calls=%async_computation.19 | async-start | bytes 5308416 | tf_op jit(solution)/shard_map/all_gather | solution.py:390
  13.9 321.1 %all-gather.23.cloned.1.call-start = ((), (), s32[]{:S(2)}) async-start(), calls=%async_computation.20 | async-start | bytes 5308416 | tf_op jit(solution)/shard_map/all_gather | solution.py:391
  25.6 48.4 %collective-permute-start.8 = (bf16[196,576]{1,0:T(8,128)(2,1)S(1)}, bf16[196,576]{1,0:T(8,128)(2,1)S(1)}, u32[]{:S(2)}, u32[]{:S(2)}) collective-permute-start(bf16[196,576]{1,0:T(8,128)(2,1)S(1)} %get-tuple-element.213), channel_id=1, source_target_pairs={{0,24},{1,25},{2,26},{3,27},{4,28},{5,29},{6,30},{7,31},{8,16},{9,... | collective-permute-start | bytes 677384 | tf_op jit(solution)/shard_map/ppermute | solution.py:255
  29.6 44.4 %collective-permute-start.6 = (bf16[196,576]{1,0:T(8,128)(2,1)S(1)}, bf16[196,576]{1,0:T(8,128)(2,1)S(1)}, u32[]{:S(2)}, u32[]{:S(2)}) collective-permute-start(bf16[196,576]{1,0:T(8,128)(2,1)S(1)} %get-tuple-element.215), channel_id=1, source_target_pairs={{0,8},{1,9},{2,10},{3,11},{4,12},{5,13},{6,14},{7,15},{8,0},{9,1},... | collective-permute-start | bytes 677384 | tf_op jit(solution)/shard_map/ppermute | solution.py:255
  30.1 43.9 %collective-permute-start.7 = (bf16[196,576]{1,0:T(8,128)(2,1)S(1)}, bf16[196,576]{1,0:T(8,128)(2,1)S(1)}, u32[]{:S(2)}, u32[]{:S(2)}) collective-permute-start(bf16[196,576]{1,0:T(8,128)(2,1)S(1)} %get-tuple-element.214), channel_id=1, source_target_pairs={{0,16},{1,17},{2,18},{3,19},{4,20},{5,21},{6,22},{7,23},{8,24},{9,... | collective-permute-start | bytes 677384 | tf_op jit(solution)/shard_map/ppermute | solution.py:255
  30.3 45.6 %collective-permute-start = (bf16[256,768]{1,0:T(8,128)(2,1)S(1)}, bf16[256,768]{1,0:T(8,128)(2,1)S(1)}, u32[]{:S(2)}, u32[]{:S(2)}) collective-permute-start(bf16[256,768]{1,0:T(8,128)(2,1)S(1)} %copy-done.99), channel_id=1, source_target_pairs={{0,0},{1,8},{2,16},{3,24},{4,4},{5,12},{6,20},{7,28},{8,1},{9,9},{... | collective-permute-start | bytes 1179656 | tf_op jit(solution)/shard_map/ppermute | solution.py:248
  31.1 29.3 %collective-permute-start.1 = (s32[1,128]{1,0:T(1,128)S(1)}, s32[1,128]{1,0:T(1,128)S(1)}, u32[]{:S(2)}, u32[]{:S(2)}) collective-permute-start(s32[1,128]{1,0:T(1,128)S(1)} %pad_bitcast_fusion), channel_id=1, source_target_pairs={{0,1},{1,0},{2,3},{3,2},{4,5},{5,4},{6,7},{7,6},{8,9},{9,8},{10,11... | collective-permute-start | bytes 1544 | tf_op jit(solution)/shard_map/ppermute | solution.py:277
  35.7 588.6 %reduce-scatter.9.cloned.1.call-start = ((), (), s32[]{:S(2)}) async-start(), calls=%async_computation.10 | async-start | bytes 1327104 | tf_op jit(solution)/shard_map/reduce_scatter | solution.py:476
  60.4 4.5 collective-permute-start.2
  82.8 20.5 %collective-permute-start.10 = (bf16[256,768]{1,0:T(8,128)(2,1)S(1)}, bf16[256,768]{1,0:T(8,128)(2,1)}, u32[]{:S(2)}, u32[]{:S(2)}) collective-permute-start(bf16[256,768]{1,0:T(8,128)(2,1)S(1)} %get-tuple-element.183), channel_id=1, source_target_pairs={{0,8},{1,9},{2,10},{3,11},{4,12},{5,13},{6,14},{7,15},{8,0},{9,1},... | collective-permute-start | bytes 1179656 | tf_op jit(solution)/shard_map/ppermute | solution.py:255
  82.8 22.3 %collective-permute-start.11 = (bf16[256,768]{1,0:T(8,128)(2,1)S(1)}, bf16[256,768]{1,0:T(8,128)(2,1)}, u32[]{:S(2)}, u32[]{:S(2)}) collective-permute-start(bf16[256,768]{1,0:T(8,128)(2,1)S(1)} %get-tuple-element.183), channel_id=1, source_target_pairs={{0,16},{1,17},{2,18},{3,19},{4,20},{5,21},{6,22},{7,23},{8,24},{9,... | collective-permute-start | bytes 1179656 | tf_op jit(solution)/shard_map/ppermute | solution.py:255
  83.7 29.4 %collective-permute-start.12 = (bf16[256,768]{1,0:T(8,128)(2,1)S(1)}, bf16[256,768]{1,0:T(8,128)(2,1)S(1)}, u32[]{:S(2)}, u32[]{:S(2)}) collective-permute-start(bf16[256,768]{1,0:T(8,128)(2,1)S(1)} %get-tuple-element.183), channel_id=1, source_target_pairs={{0,24},{1,25},{2,26},{3,27},{4,28},{5,29},{6,30},{7,31},{8,16},{9,... | collective-permute-start | bytes 1179656 | tf_op jit(solution)/shard_map/ppermute | solution.py:255
  118.2 17.3 %collective-permute-start.14 = (bf16[1024,384]{1,0:T(8,128)(2,1)}, bf16[1024,384]{1,0:T(8,128)(2,1)}, u32[]{:S(2)}, u32[]{:S(2)}) collective-permute-start(bf16[1024,384]{1,0:T(8,128)(2,1)} %fusion.61), channel_id=1, source_target_pairs={{0,4},{1,5},{2,6},{3,7},{4,1},{5,2},{6,3},{8,12},{9,13},{10,14},{1... | collective-permute-start | bytes 2359304 | tf_op jit(solution)/shard_map/ppermute | solution.py:263
  123.0 12.4 %collective-permute-start.13 = (bf16[512,384]{1,0:T(8,128)(2,1)}, bf16[512,384]{1,0:T(8,128)(2,1)S(1)}, u32[]{:S(2)}, u32[]{:S(2)}) collective-permute-start(bf16[512,384]{1,0:T(8,128)(2,1)} %get-tuple-element.219), channel_id=1, source_target_pairs={{0,1},{1,2},{2,3},{4,5},{5,6},{6,7},{8,9},{9,10},{10,11},{12,13},{... | collective-permute-start | bytes 1179656 | tf_op jit(solution)/shard_map/ppermute | solution.py:263
  126.5 10.8 %collective-permute-start.15 = (bf16[1024,384]{1,0:T(8,128)(2,1)}, bf16[1024,384]{1,0:T(8,128)(2,1)S(1)}, u32[]{:S(2)}, u32[]{:S(2)}) collective-permute-start(bf16[1024,384]{1,0:T(8,128)(2,1)} %fusion.61), channel_id=1, source_target_pairs={{1,4},{2,5},{3,6},{4,0},{5,1},{6,2},{7,3},{9,12},{10,13},{11,14},{... | collective-permute-start | bytes 2359304 | tf_op jit(solution)/shard_map/ppermute | solution.py:263
  127.8 22.1 %collective-permute-start.16 = (bf16[512,384]{1,0:T(8,128)(2,1)}, bf16[512,384]{1,0:T(8,128)(2,1)S(1)}, u32[]{:S(2)}, u32[]{:S(2)}) collective-permute-start(bf16[512,384]{1,0:T(8,128)(2,1)} %get-tuple-element.218), channel_id=1, source_target_pairs={{1,0},{2,1},{3,2},{5,4},{6,5},{7,6},{9,8},{10,9},{11,10},{13,12},{... | collective-permute-start | bytes 1179656 | tf_op jit(solution)/shard_map/ppermute | solution.py:263
  177.3 5.9 collective-permute-start.17
  177.9 5.3 collective-permute-start.18
  178.5 5.9 collective-permute-start.19
  203.1 18.4 %collective-permute-start.20 = (bf16[256,768]{1,0:T(8,128)(2,1)S(1)}, bf16[256,768]{1,0:T(8,128)(2,1)S(1)}, u32[]{:S(2)}, u32[]{:S(2)}) collective-permute-start(bf16[256,768]{1,0:T(8,128)(2,1)S(1)} %get-tuple-element.181), channel_id=1, source_target_pairs={{0,8},{1,9},{2,10},{3,11},{4,12},{5,13},{6,14},{7,15},{8,0},{9,1},... | collective-permute-start | bytes 1179656 | tf_op jit(solution)/shard_map/ppermute | solution.py:255
  204.5 17.9 %collective-permute-start.21 = (bf16[256,768]{1,0:T(8,128)(2,1)S(1)}, bf16[256,768]{1,0:T(8,128)(2,1)S(1)}, u32[]{:S(2)}, u32[]{:S(2)}) collective-permute-start(bf16[256,768]{1,0:T(8,128)(2,1)S(1)} %get-tuple-element.181), channel_id=1, source_target_pairs={{0,16},{1,17},{2,18},{3,19},{4,20},{5,21},{6,22},{7,23},{8,24},{9,... | collective-permute-start | bytes 1179656 | tf_op jit(solution)/shard_map/ppermute | solution.py:255
  206.0 24.3 %collective-permute-start.22 = (bf16[256,768]{1,0:T(8,128)(2,1)S(1)}, bf16[256,768]{1,0:T(8,128)(2,1)S(1)}, u32[]{:S(2)}, u32[]{:S(2)}) collective-permute-start(bf16[256,768]{1,0:T(8,128)(2,1)S(1)} %get-tuple-element.181), channel_id=1, source_target_pairs={{0,24},{1,25},{2,26},{3,27},{4,28},{5,29},{6,30},{7,31},{8,16},{9,... | collective-permute-start | bytes 1179656 | tf_op jit(solution)/shard_map/ppermute | solution.py:255
  233.9 17.3 %collective-permute-start.24 = (bf16[1024,384]{1,0:T(8,128)(2,1)S(1)}, bf16[1024,384]{1,0:T(8,128)(2,1)S(1)}, u32[]{:S(2)}, u32[]{:S(2)}) collective-permute-start(bf16[1024,384]{1,0:T(8,128)(2,1)S(1)} %fusion.60), channel_id=1, source_target_pairs={{0,4},{1,5},{2,6},{3,7},{4,1},{5,2},{6,3},{8,12},{9,13},{10,14},{1... | collective-permute-start | bytes 2359304 | tf_op jit(solution)/shard_map/ppermute | solution.py:263
  236.2 14.2 %collective-permute-start.23 = (bf16[512,384]{1,0:T(8,128)(2,1)}, bf16[512,384]{1,0:T(8,128)(2,1)S(1)}, u32[]{:S(2)}, u32[]{:S(2)}) collective-permute-start(bf16[512,384]{1,0:T(8,128)(2,1)} %get-tuple-element.217), channel_id=1, source_target_pairs={{0,1},{1,2},{2,3},{4,5},{5,6},{6,7},{8,9},{9,10},{10,11},{12,13},{... | collective-permute-start | bytes 1179656 | tf_op jit(solution)/shard_map/ppermute | solution.py:263
  240.5 94.4 %collective-permute-start.31 = (bf16[256,768]{1,0:T(8,128)(2,1)}, bf16[256,768]{1,0:T(8,128)(2,1)S(1)}, u32[]{:S(2)}, u32[]{:S(2)}) collective-permute-start(bf16[256,768]{1,0:T(8,128)(2,1)} %param.31), channel_id=1, source_target_pairs={{0,0},{1,8},{2,16},{3,24},{4,4},{5,12},{6,20},{7,28},{8,1},{9,9},{... | collective-permute-start | bytes 1179656 | tf_op jit(solution)/shard_map/ppermute | solution.py:248
  244.5 9.0 collective-permute-start.25
  246.2 42.1 %collective-permute-start.26 = (bf16[512,384]{1,0:T(8,128)(2,1)}, bf16[512,384]{1,0:T(8,128)(2,1)S(1)}, u32[]{:S(2)}, u32[]{:S(2)}) collective-permute-start(bf16[512,384]{1,0:T(8,128)(2,1)} %get-tuple-element.216), channel_id=1, source_target_pairs={{1,0},{2,1},{3,2},{5,4},{6,5},{7,6},{9,8},{10,9},{11,10},{13,12},{... | collective-permute-start | bytes 1179656 | tf_op jit(solution)/shard_map/ppermute | solution.py:263
  314.8 5.0 collective-permute-start.27
  314.9 5.0 collective-permute-start.28
  314.9 6.4 collective-permute-start.29
  346.3 4.7 collective-permute-start.32
  348.3 4.6 collective-permute-start.33
  349.8 5.5 collective-permute-start.34
  382.2 20.3 %collective-permute-start.35 = (bf16[1024,384]{1,0:T(8,128)(2,1)S(1)}, bf16[1024,384]{1,0:T(8,128)(2,1)S(1)}, u32[]{:S(2)}, u32[]{:S(2)}) collective-permute-start(bf16[1024,384]{1,0:T(8,128)(2,1)S(1)} %get-tuple-element.190), channel_id=1, source_target_pairs={{1,4},{2,5},{3,6},{4,0},{5,1},{6,2},{7,3},{9,12},{10,13},{11,14},{... | collective-permute-start | bytes 2359304 | tf_op jit(solution)/shard_map/ppermute | solution.py:263
  383.6 18.9 %collective-permute-start.36 = (bf16[1024,384]{1,0:T(8,128)(2,1)S(1)}, bf16[1024,384]{1,0:T(8,128)(2,1)S(1)}, u32[]{:S(2)}, u32[]{:S(2)}) collective-permute-start(bf16[1024,384]{1,0:T(8,128)(2,1)S(1)} %get-tuple-element.191), channel_id=1, source_target_pairs={{0,4},{1,5},{2,6},{3,7},{4,1},{5,2},{6,3},{8,12},{9,13},{10,14},{1... | collective-permute-start | bytes 2359304 | tf_op jit(solution)/shard_map/ppermute | solution.py:263
  386.8 27.6 %collective-permute-start.37 = (bf16[512,384]{1,0:T(8,128)(2,1)S(1)}, bf16[512,384]{1,0:T(8,128)(2,1)S(1)}, u32[]{:S(2)}, u32[]{:S(2)}) collective-permute-start(bf16[512,384]{1,0:T(8,128)(2,1)S(1)} %get-tuple-element.189), channel_id=1, source_target_pairs={{1,0},{2,1},{3,2},{5,4},{6,5},{7,6},{9,8},{10,9},{11,10},{13,12},{... | collective-permute-start | bytes 1179656 | tf_op jit(solution)/shard_map/ppermute | solution.py:263
  388.1 26.4 %collective-permute-start.38 = (bf16[512,384]{1,0:T(8,128)(2,1)S(1)}, bf16[512,384]{1,0:T(8,128)(2,1)S(1)}, u32[]{:S(2)}, u32[]{:S(2)}) collective-permute-start(bf16[512,384]{1,0:T(8,128)(2,1)S(1)} %get-tuple-element.188), channel_id=1, source_target_pairs={{0,1},{1,2},{2,3},{4,5},{5,6},{6,7},{8,9},{9,10},{10,11},{12,13},{... | collective-permute-start | bytes 1179656 | tf_op jit(solution)/shard_map/ppermute | solution.py:263
  418.4 12.3 %collective-permute-start.39 = (bf16[256,768]{1,0:T(8,128)(2,1)}, bf16[256,768]{1,0:T(8,128)(2,1)}, u32[]{:S(2)}, u32[]{:S(2)}) collective-permute-start(bf16[256,768]{1,0:T(8,128)(2,1)} %get-tuple-element.203), channel_id=1, source_target_pairs={{0,8},{1,9},{2,10},{3,11},{4,12},{5,13},{6,14},{7,15},{8,0},{9,1},... | collective-permute-start | bytes 1179656 | tf_op jit(solution)/shard_map/ppermute | solution.py:255
  420.0 20.3 %collective-permute-start.40 = (bf16[256,768]{1,0:T(8,128)(2,1)}, bf16[256,768]{1,0:T(8,128)(2,1)}, u32[]{:S(2)}, u32[]{:S(2)}) collective-permute-start(bf16[256,768]{1,0:T(8,128)(2,1)} %get-tuple-element.205), channel_id=1, source_target_pairs={{0,16},{1,17},{2,18},{3,19},{4,20},{5,21},{6,22},{7,23},{8,24},{9,... | collective-permute-start | bytes 1179656 | tf_op jit(solution)/shard_map/ppermute | solution.py:255
  420.5 19.8 %collective-permute-start.41 = (bf16[256,768]{1,0:T(8,128)(2,1)}, bf16[256,768]{1,0:T(8,128)(2,1)}, u32[]{:S(2)}, u32[]{:S(2)}) collective-permute-start(bf16[256,768]{1,0:T(8,128)(2,1)} %get-tuple-element.204), channel_id=1, source_target_pairs={{0,24},{1,25},{2,26},{3,27},{4,28},{5,29},{6,30},{7,31},{8,16},{9,... | collective-permute-start | bytes 1179656 | tf_op jit(solution)/shard_map/ppermute | solution.py:255
  423.6 200.7 %reduce-scatter.7.cloned.1.call-start = ((), (), s32[]{:S(2)}) async-start(), calls=%async_computation.9 | async-start | bytes 1327104 | tf_op jit(solution)/shard_map/reduce_scatter | solution.py:476
  454.4 169.9 %reduce-scatter.13.cloned.1.call-start = ((), (), s32[]{:S(2)}) async-start(), calls=%async_computation.12 | async-start | bytes 5308416 | tf_op jit(solution)/shard_map/reduce_scatter | solution.py:477
  459.8 178.8 %reduce-scatter.17.cloned.1.call-start = ((), (), s32[]{:S(2)}) async-start(), calls=%async_computation.14 | async-start | bytes 5308416 | tf_op jit(solution)/shard_map/reduce_scatter | solution.py:478
  465.1 230.8 %reduce-scatter.15.cloned.1.call-start = ((), (), s32[]{:S(2)}) async-start(), calls=%async_computation.13 | async-start | bytes 5308416 | tf_op jit(solution)/shard_map/reduce_scatter | solution.py:478
  470.3 282.6 %reduce-scatter.11.cloned.1.call-start = ((), (), s32[]{:S(2)}) async-start(), calls=%async_computation.11 | async-start | bytes 5308416 | tf_op jit(solution)/shard_map/reduce_scatter | solution.py:477
  490.1 67.3 %all-to-all-start.1 = ((bf16[8,96,576]{2,1,0:T(8,128)(2,1)}), bf16[8,96,576]{2,1,0:T(8,128)(2,1)}, u32[]{:S(2)}, u32[]{:S(2)}) async-start(bf16[8,96,576]{2,1,0:T(8,128)(2,1)} %bitcast.78), calls=%async_computation.1 | async-start | bytes 1966080 | tf_op jit(solution)/shard_map/all_to_all | solution.py:471
  497.2 15.2 %collective-permute-start.42 = (bf16[256,192]{0,1:T(8,128)(2,1)S(1)}, bf16[256,192]{0,1:T(8,128)(2,1)S(1)}, u32[]{:S(2)}, u32[]{:S(2)}) collective-permute-start(bf16[256,192]{0,1:T(8,128)(2,1)S(1)} %get-tuple-element.246), channel_id=1, source_target_pairs={{0,8},{1,9},{2,10},{3,11},{4,12},{5,13},{6,14},{7,15},{8,0},{9,1},... | collective-permute-start | bytes 294920 | tf_op jit(solution)/shard_map/ppermute | solution.py:255
  499.2 13.2 %collective-permute-start.43 = (bf16[256,192]{0,1:T(8,128)(2,1)S(1)}, bf16[256,192]{0,1:T(8,128)(2,1)S(1)}, u32[]{:S(2)}, u32[]{:S(2)}) collective-permute-start(bf16[256,192]{0,1:T(8,128)(2,1)S(1)} %get-tuple-element.245), channel_id=1, source_target_pairs={{0,16},{1,17},{2,18},{3,19},{4,20},{5,21},{6,22},{7,23},{8,24},{9,... | collective-permute-start | bytes 294920 | tf_op jit(solution)/shard_map/ppermute | solution.py:255
  500.7 14.2 %collective-permute-start.44 = (bf16[256,192]{0,1:T(8,128)(2,1)S(1)}, bf16[256,192]{0,1:T(8,128)(2,1)S(1)}, u32[]{:S(2)}, u32[]{:S(2)}) collective-permute-start(bf16[256,192]{0,1:T(8,128)(2,1)S(1)} %get-tuple-element.244), channel_id=1, source_target_pairs={{0,24},{1,25},{2,26},{3,27},{4,28},{5,29},{6,30},{7,31},{8,16},{9,... | collective-permute-start | bytes 294920 | tf_op jit(solution)/shard_map/ppermute | solution.py:255
  543.3 24.0 %collective-permute-start.45 = (bf16[1024,384]{1,0:T(8,128)(2,1)}, bf16[1024,384]{1,0:T(8,128)(2,1)}, u32[]{:S(2)}, u32[]{:S(2)}) collective-permute-start(bf16[1024,384]{1,0:T(8,128)(2,1)} %get-tuple-element.186), channel_id=1, source_target_pairs={{1,4},{2,5},{3,6},{4,0},{5,1},{6,2},{7,3},{9,12},{10,13},{11,14},{... | collective-permute-start | bytes 2359304 | tf_op jit(solution)/shard_map/ppermute | solution.py:263
  544.6 22.7 %collective-permute-start.46 = (bf16[1024,384]{1,0:T(8,128)(2,1)}, bf16[1024,384]{1,0:T(8,128)(2,1)}, u32[]{:S(2)}, u32[]{:S(2)}) collective-permute-start(bf16[1024,384]{1,0:T(8,128)(2,1)} %get-tuple-element.187), channel_id=1, source_target_pairs={{0,4},{1,5},{2,6},{3,7},{4,1},{5,2},{6,3},{8,12},{9,13},{10,14},{1... | collective-permute-start | bytes 2359304 | tf_op jit(solution)/shard_map/ppermute | solution.py:263
  550.6 18.7 %collective-permute-start.47 = (bf16[512,384]{1,0:T(8,128)(2,1)}, bf16[512,384]{1,0:T(8,128)(2,1)}, u32[]{:S(2)}, u32[]{:S(2)}) collective-permute-start(bf16[512,384]{1,0:T(8,128)(2,1)} %get-tuple-element.185), channel_id=1, source_target_pairs={{1,0},{2,1},{3,2},{5,4},{6,5},{7,6},{9,8},{10,9},{11,10},{13,12},{... | collective-permute-start | bytes 1179656 | tf_op jit(solution)/shard_map/ppermute | solution.py:263
  551.9 18.6 %collective-permute-start.48 = (bf16[512,384]{1,0:T(8,128)(2,1)}, bf16[512,384]{1,0:T(8,128)(2,1)}, u32[]{:S(2)}, u32[]{:S(2)}) collective-permute-start(bf16[512,384]{1,0:T(8,128)(2,1)} %get-tuple-element.184), channel_id=1, source_target_pairs={{0,1},{1,2},{2,3},{4,5},{5,6},{6,7},{8,9},{9,10},{10,11},{12,13},{... | collective-permute-start | bytes 1179656 | tf_op jit(solution)/shard_map/ppermute | solution.py:263
  574.3 14.6 %collective-permute-start.49 = (bf16[256,768]{1,0:T(8,128)(2,1)}, bf16[256,768]{1,0:T(8,128)(2,1)S(1)}, u32[]{:S(2)}, u32[]{:S(2)}) collective-permute-start(bf16[256,768]{1,0:T(8,128)(2,1)} %get-tuple-element.200), channel_id=1, source_target_pairs={{0,8},{1,9},{2,10},{3,11},{4,12},{5,13},{6,14},{7,15},{8,0},{9,1},... | collective-permute-start | bytes 1179656 | tf_op jit(solution)/shard_map/ppermute | solution.py:255
  574.7 17.6 %collective-permute-start.50 = (bf16[256,768]{1,0:T(8,128)(2,1)}, bf16[256,768]{1,0:T(8,128)(2,1)}, u32[]{:S(2)}, u32[]{:S(2)}) collective-permute-start(bf16[256,768]{1,0:T(8,128)(2,1)} %get-tuple-element.202), channel_id=1, source_target_pairs={{0,16},{1,17},{2,18},{3,19},{4,20},{5,21},{6,22},{7,23},{8,24},{9,... | collective-permute-start | bytes 1179656 | tf_op jit(solution)/shard_map/ppermute | solution.py:255
  574.9 23.6 %collective-permute-start.51 = (bf16[256,768]{1,0:T(8,128)(2,1)}, bf16[256,768]{1,0:T(8,128)(2,1)}, u32[]{:S(2)}, u32[]{:S(2)}) collective-permute-start(bf16[256,768]{1,0:T(8,128)(2,1)} %get-tuple-element.201), channel_id=1, source_target_pairs={{0,24},{1,25},{2,26},{3,27},{4,28},{5,29},{6,30},{7,31},{8,16},{9,... | collective-permute-start | bytes 1179656 | tf_op jit(solution)/shard_map/ppermute | solution.py:255
  585.0 33.2 %all-to-all-start = ((bf16[8,96,576]{2,1,0:T(8,128)(2,1)}), bf16[8,96,576]{2,1,0:T(8,128)(2,1)S(1)}, u32[]{:S(2)}, u32[]{:S(2)}) async-start(bf16[8,96,576]{2,1,0:T(8,128)(2,1)} %bitcast.69), calls=%async_computation | async-start | bytes 1966080 | tf_op jit(solution)/shard_map/all_to_all | solution.py:471
  588.5 314.7 %all-reduce.6.cloned.1.call-start = ((), (), s32[]{:S(2)}) async-start(), calls=%async_computation.8 | async-start | bytes 147456 | tf_op jit(solution)/shard_map/psum | solution.py:506
  602.7 440.0 %all-reduce.8.cloned.1.call-start = ((), (), s32[]{:S(2)}) async-start(), calls=%async_computation.21 | async-start | bytes 7077888 | tf_op jit(solution)/shard_map/psum | solution.py:504
  762.9 144.4 %collective-permute-start.52 = (bf16[256,768]{1,0:T(8,128)(2,1)S(1)}, bf16[256,768]{1,0:T(8,128)(2,1)S(1)}, u32[]{:S(2)}, u32[]{:S(2)}) collective-permute-start(bf16[256,768]{1,0:T(8,128)(2,1)S(1)} %fusion.101), channel_id=1, source_target_pairs={{0,0},{8,1},{16,2},{24,3},{4,4},{12,5},{20,6},{28,7},{1,8},{9,9},{... | collective-permute-start | bytes 1179656 | tf_op jit(solution)/shard_map/ppermute | solution.py:251
  (108 other events, 1249.6 us)
Sparse Core Ops, SparseCore 0:
  9.9 33.5 all-gather.12
  45.9 61.0 all-gather.14
  108.9 42.8 all-gather.16
  153.5 24.7 all-gather.18
  180.6 51.4 all-gather.20
  233.9 49.3 all-gather.22
  423.8 37.2 reduce-scatter.8
  464.3 38.1 reduce-scatter.6
  506.0 56.4 reduce-scatter.12
  565.7 72.8 reduce-scatter.16
  642.1 53.7 reduce-scatter.14
  699.2 53.7 reduce-scatter.10
  759.1 144.0 all-reduce.5
  906.6 136.0 all-reduce.7
